TPU v7x, 512 devices: a whole 4x4x16 slice. The times are simulated.
512 devices in a mesh: seq: 64 (over x, z), head: 8 (over y, core).
Axes of the slice: x: 4, y: 4, z: 16, core: 2. Of those that a mesh axis runs over, the one named last changes fastest.
Arguments:
- query_raw: bfloat16 [24576, 2048], P('seq', 'head'), may hold values from -6 to 6
- key_raw: bfloat16 [24576, 2048], P('seq', 'head'), may hold values from -6 to 6
- value_raw: bfloat16 [24576, 4096], P('seq', 'head'), may hold values from -6 to 6
- gate_raw: bfloat16 [24576, 4096], P('seq', 'head'), may hold values from -6 to 6
- query_taps: float32 [4, 2048], P(None, 'head'), may hold values from -3 to 3
- key_taps: float32 [4, 2048], P(None, 'head'), may hold values from -3 to 3
- value_taps: float32 [4, 4096], P(None, 'head'), may hold values from -3 to 3
- beta_logit: float32 [24576, 32], P('seq', 'head'), may hold values from -6 to 6
- decay_logit: float32 [24576, 32], P('seq', 'head'), may hold values from -14 to 0
- norm_gain: float32 [128], replicated, may hold values from 0.5 to 1.5
- out_weight: bfloat16 [4096, 2048], P('head'), may hold values from -0.09375 to 0.09375
Outputs:
- mixed: bfloat16 [24576, 2048], P(('seq', 'head'))
All inputs are finite; a program needn't handle non-finite values.
Results may differ from a plain program's by a relative error of at most 0.017.
Values may be sent and summed in bfloat16 or wider, within the bound.
A program may use at most 128 MiB of HBM per device.

v0:
```python
import jax
import jax.numpy as jnp
from jax import lax
from jax.sharding import PartitionSpec as P

DK = 128
DV = 128
BLOCK = 64


PRECISE = lax.Precision.HIGHEST
EPSILON = 1e-06


def passed_along(value, axis, by):
    count = lax.axis_size(axis)
    pairs = [(i, i + by) for i in range(count) if 0 <= i + by < count]
    return lax.ppermute(value, axis, pairs)


def carried_in(part, axis, combine, identity):
    place = lax.axis_index(axis)
    gathered = jax.tree.map(lambda a: lax.all_gather(a, axis), part)
    state = jax.tree.map(lambda a, e: jnp.zeros_like(a) + jnp.asarray(e, a.dtype), part, identity)

    def one(hop, state):
        return combine(
            state, jax.tree.map(lambda a: lax.dynamic_index_in_dim(a, hop, 0, False), gathered)
        )

    return lax.fori_loop(0, place, one, state)


def conv_silu(raw_rows, before, weight):
    extended = jnp.concatenate([before, raw_rows], 0).astype(jnp.float32)
    length = raw_rows.shape[0]
    summed = weight[0] * extended[0:length]
    for offset in range(1, 4):
        summed = summed + weight[offset] * extended[offset : offset + length]
    return jax.nn.silu(summed)


def prepare(query_conv, key_conv, value_conv, beta_logit, decay_logit):
    length = query_conv.shape[0]
    head_keys = key_conv.shape[1] // DK
    head_values = value_conv.shape[1] // DV
    repeat_by = head_values // head_keys
    blocks = length // BLOCK
    key_three = key_conv.reshape(length, head_keys, DK)
    key_three = key_three * lax.rsqrt(jnp.sum(key_three * key_three, -1, keepdims=True) + EPSILON)
    query_three = query_conv.reshape(length, head_keys, DK)

    def arrange(array_in):
        moved = jnp.moveaxis(array_in, 1, 0)
        return moved.reshape((moved.shape[0], blocks, BLOCK) + moved.shape[2:])

    queries = arrange(jnp.repeat(query_three, repeat_by, axis=1))
    key_rows = arrange(jnp.repeat(key_three, repeat_by, axis=1))
    value_rows = arrange(value_conv.reshape(length, head_values, DV))
    decays = arrange(-jax.nn.softplus(decay_logit))
    beta_rows = arrange(jax.nn.sigmoid(beta_logit))
    return (queries, key_rows, value_rows, decays, beta_rows)


def stack_mul(left, right):
    return jnp.einsum("bkl,blv->bkv", left, right, precision=PRECISE)


def block_parts(queries, key_rows, value_rows, decays, beta_rows):
    block_len = decays.shape[-1]
    log_fade = jnp.cumsum(decays, axis=-1)
    row_ids = lax.broadcasted_iota(jnp.int32, (block_len, block_len), 0)
    col_ids = lax.broadcasted_iota(jnp.int32, (block_len, block_len), 1)
    gap_log = log_fade[..., :, None] - log_fade[..., None, :]
    strict = row_ids > col_ids
    within = row_ids >= col_ids
    decay_low = jnp.where(strict, jnp.exp(jnp.where(strict, gap_log, 0.0)), 0.0)
    decay_on = jnp.where(within, jnp.exp(jnp.where(within, gap_log, 0.0)), 0.0)
    key_inner = jnp.einsum("bik,bjk->bij", key_rows, key_rows, precision=PRECISE)
    system = jnp.eye(block_len, dtype=jnp.float32) + beta_rows[..., :, None] * decay_low * key_inner
    rhs_both = jnp.concatenate(
        [beta_rows[..., None] * value_rows, (beta_rows * jnp.exp(log_fade))[..., None] * key_rows],
        -1,
    )
    solved = lax.linalg.triangular_solve(
        system, rhs_both, left_side=True, lower=True, unit_diagonal=True
    )
    value_dim = value_rows.shape[-1]
    updates = solved[..., :value_dim]
    wide = solved[..., value_dim:]
    scores = decay_on * jnp.einsum("bik,bjk->bij", queries, key_rows, precision=PRECISE)
    tail_fade = jnp.exp(log_fade[..., -1:] - log_fade)
    faded_keys = key_rows * tail_fade[..., None]
    last_fade = jnp.exp(log_fade[..., -1])
    identity = jnp.eye(key_rows.shape[-1], dtype=jnp.float32)
    transit = last_fade[..., None, None] * identity - jnp.einsum(
        "bck,bcl->bkl", faded_keys, wide, precision=PRECISE
    )
    inject = jnp.einsum("bck,bcv->bkv", faded_keys, updates, precision=PRECISE)
    return (updates, wide, scores, log_fade, transit, inject)


def block_out(queries, scores, log_fade, updates, wide, state_now):
    fresh = updates - jnp.einsum("bck,bkv->bcv", wide, state_now, precision=PRECISE)
    carried = jnp.einsum("bck,bkv->bcv", queries, state_now, precision=PRECISE)
    return jnp.exp(log_fade)[..., None] * carried + jnp.einsum(
        "bij,bjv->biv", scores, fresh, precision=PRECISE
    )


def gated_norm(outputs, gate_raw, norm_gain):
    gate_three = gate_raw.reshape(outputs.shape).astype(jnp.float32)
    scale_rows = lax.rsqrt(jnp.mean(outputs * outputs, -1, keepdims=True) + EPSILON)
    normed = (outputs * scale_rows * norm_gain * jax.nn.silu(gate_three)).astype(jnp.bfloat16)
    return normed.reshape(outputs.shape[0], -1)


def shards(
    query_raw,
    key_raw,
    value_raw,
    gate_raw,
    query_taps,
    key_taps,
    value_taps,
    beta_logit,
    decay_logit,
    norm_gain,
    out_weight,
):
    before = passed_along((query_raw[-3:], key_raw[-3:], value_raw[-3:]), "seq", 1)
    query_conv = conv_silu(query_raw, before[0], query_taps)
    key_conv = conv_silu(key_raw, before[1], key_taps)
    value_conv = conv_silu(value_raw, before[2], value_taps)
    prepared = prepare(query_conv, key_conv, value_conv, beta_logit, decay_logit)
    heads_here = prepared[0].shape[0]
    blocks = prepared[0].shape[1]
    flattened = tuple(
        (array_in.reshape((heads_here * blocks,) + array_in.shape[2:]) for array_in in prepared)
    )
    updates, wide, scores, log_fade, transit, inject = block_parts(
        flattened[0], flattened[1], flattened[2], flattened[3], flattened[4]
    )
    transit_seq = jnp.moveaxis(transit.reshape(heads_here, blocks, DK, DK), 1, 0)
    inject_seq = jnp.moveaxis(inject.reshape(heads_here, blocks, DK, DV), 1, 0)

    def compose(running, pair_now):
        return (
            (stack_mul(pair_now[0], running[0]), stack_mul(pair_now[0], running[1]) + pair_now[1]),
            None,
        )

    identity = jnp.broadcast_to(jnp.eye(DK, dtype=jnp.float32), (heads_here, DK, DK))
    empty_state = jnp.zeros((heads_here, DK, DV), jnp.float32)
    (device_m, device_h), _ = lax.scan(compose, (identity, empty_state), (transit_seq, inject_seq))

    def combine(earlier_pair, later_pair):
        return (
            stack_mul(later_pair[0], earlier_pair[0]),
            stack_mul(later_pair[0], earlier_pair[1]) + later_pair[1],
        )

    prefix = carried_in((device_m, device_h), "seq", combine, (identity, empty_state))
    state_in = prefix[1]

    def advance(state_now, pair_now):
        return (stack_mul(pair_now[0], state_now) + pair_now[1], state_now)

    _, starts = lax.scan(advance, state_in, (transit_seq, inject_seq))
    starts = jnp.moveaxis(starts, 0, 1).reshape(heads_here * blocks, DK, DV)
    outputs = block_out(flattened[0], scores, log_fade, updates, wide, starts)
    core = jnp.moveaxis(outputs.reshape(heads_here, -1, DV), 0, 1)
    normed = gated_norm(core, gate_raw, norm_gain)
    return lax.psum_scatter(
        jnp.dot(normed, out_weight, preferred_element_type=jnp.float32).astype(jnp.bfloat16),
        "head",
        scatter_dimension=0,
        tiled=True,
    )


def solution(mesh):
    placed = (
        P("seq", "head"),
        P("seq", "head"),
        P("seq", "head"),
        P("seq", "head"),
        P(None, "head"),
        P(None, "head"),
        P(None, "head"),
        P("seq", "head"),
        P("seq", "head"),
        P(),
        P("head", None),
    )
    return jax.shard_map(
        shards, mesh=mesh, in_specs=placed, out_specs=P(("seq", "head"), None), check_vma=False
    )
```

profile of v0, /device:TPU:1, one launch (start us, length us, event | category | flops | bytes accessed | tf_op | source)
XLA Modules:
  0.0 718.9 jit_solution(7793492137039995514)
XLA Ops:
  7.4 4.4 collective-permute-start.1
  12.5 3.5 collective-permute-start.2
  22.5 2.3 fusion.24
  24.8 119.3 %custom-call.3 = f32[24,1,64,64]{2,3,1,0:T(8,128)} custom-call(f32[24,1,64,64]{3,2,1,0:T(8,128)} %fusion.24), custom_call_target="InvertDiagBlocksLowerTriangular" | custom-call | tf_op jit(solution)/shard_map/triangular_solve | solution.py:85
  146.8 1.6 fusion.17
  148.4 2.9 fusion.38
  152.6 3.0 multiply_subtract_fusion
  156.9 17.2 %while.39 = (s32[]{:T(128)}, f32[4,128,128]{2,1,0:T(8,128)S(1)}, f32[4,128,128]{2,1,0:T(8,128)S(1)}, f32[6,4,128,128]{3,2,1,0:T(8,128)}, f32[6,4,128,128]{3,2,1,0:T(8,128)}, /*index=5*/s32[]{:T(128)}, s32[]{:T(128)}) while((s32[]{:T(128)}, f32[4,128,128]{2,1,0:T(8,128)S(1)}, f32[4,128,128]{2,1,0:T(8,128)S(1)}, ...), condition=%wide.region_3.4_spmd.clone, body=%wide.region_2.3_spmd.clone.sunk | while | flops 201457664 | bytes 2885207 | solution.py:155
  157.0 1.4 convolution_add_fusion.9
  159.8 1.4 convolution_add_fusion.9
  162.7 1.4 convolution_add_fusion.9
  165.5 1.4 convolution_add_fusion.9
  168.4 1.4 convolution_add_fusion.9
  176.3 3.8 collective-permute-start
  180.1 2.1 copy.37
  183.5 2.2 convolution_multiply_fusion
  185.7 185.7 %all-gather.5.cloned.1.call-done = f32[256,128,128]{2,1,0:T(8,128)} async-done(((f32[4,128,128]{2,1,0:T(8,128)}), f32[256,128,128]{2,1,0:T(8,128)}) %all-gather.5.cloned.1.call-update) | async-done | bytes 16777232 | tf_op jit(solution)/shard_map/all_gather | solution.py:23
  371.4 193.0 %all-gather.7.cloned.1.call-done = f32[256,128,128]{2,1,0:T(8,128)} async-done(((f32[4,128,128]{2,1,0:T(8,128)}), f32[256,128,128]{2,1,0:T(8,128)}) %all-gather.7.cloned.1.call-update) | async-done | bytes 16777232 | tf_op jit(solution)/shard_map/all_gather | solution.py:23
  564.5 13.2 %while.38 = (s32[]{:T(128)}, f32[4,128,128]{2,1,0:T(8,128)S(1)}, f32[6,4,128,128]{3,2,0,1:T(8,128)}, f32[6,4,128,128]{3,2,1,0:T(8,128)}, f32[6,4,128,128]{3,2,1,0:T(8,128)}, /*index=5*/s32[]{:T(128)}) while((s32[]{:T(128)}, f32[4,128,128]{2,1,0:T(8,128)S(1)}, f32[6,4,128,128]{3,2,0,1:T(8,128)}, f32[6,4,128,128]{3,2,1,0:T(8,128)}, ...), condition=%wide.region_7.8_spmd, body=%wide.region_6.7_spmd.sunk | while | flops 100728832 | bytes 2098757 | solution.py:169
  577.7 3.5 convolution_subtract_fusion
  581.2 1.6 convolution_multiply_fusion.1
  582.9 1.9 convolution_add_fusion.3
  587.7 2.2 convolution_convert_fusion
  589.9 122.5 %reduce-scatter.2.cloned.1.call-done = bf16[48,2048]{1,0:T(8,128)(2,1)} async-done(((bf16[384,2048]{1,0:T(8,128)(2,1)}), bf16[48,2048]{1,0:T(8,128)(2,1)}) %reduce-scatter.2.cloned.1.call-update) | async-done | bytes 196624 | tf_op jit(solution)/shard_map/reduce_scatter | solution.py:174
  (114 shorter events, 42.4 us)
Async XLA Ops:
  6.5 581.1 %copy-start = (bf16[512,2048]{1,0:T(8,128)(2,1)S(1)}, bf16[512,2048]{1,0:T(8,128)(2,1)}, u32[]{:S(2)}) copy-start(bf16[512,2048]{1,0:T(8,128)(2,1)} %param.27) | copy-start | bytes 6291460
  6.5 364.9 %all-gather.5.cloned.1.call-start = ((), (), s32[]{:S(2)}) async-start(), calls=%async_computation.2 | async-start | bytes 17039360 | tf_op jit(solution)/shard_map/all_gather | solution.py:23
  7.4 12.5 %collective-permute-start.1 = (bf16[3,256]{1,0:T(4,128)(2,1)S(1)}, bf16[3,256]{1,0:T(4,128)(2,1)S(1)}, u32[]{:S(2)}, u32[]{:S(2)}) collective-permute-start(bf16[3,256]{1,0:T(4,128)(2,1)S(1)} %slice.106), channel_id=1, source_target_pairs={{0,8},{8,16},{16,24},{24,32},{32,40},{40,48},{48,56},{56,64},{64,7... | collective-permute-start | bytes 4616 | tf_op jit(solution)/shard_map/ppermute | solution.py:18
  12.5 131.6 %collective-permute-start.2 = (bf16[3,512]{1,0:T(4,128)(2,1)S(1)}, bf16[3,512]{1,0:T(4,128)(2,1)S(1)}, u32[]{:S(2)}, u32[]{:S(2)}) collective-permute-start(bf16[3,512]{1,0:T(4,128)(2,1)S(1)} %slice.115), channel_id=1, source_target_pairs={{0,8},{8,16},{16,24},{24,32},{32,40},{40,48},{48,56},{56,64},{64,7... | collective-permute-start | bytes 9224 | tf_op jit(solution)/shard_map/ppermute | solution.py:18
  145.7 1.1 copy-start.8
  148.4 4.2 copy-start.2
  156.9 23.2 %copy-start.10 = (f32[4,256]{1,0:T(4,128)S(1)}, f32[4,256]{1,0:T(4,128)}, u32[]{:S(2)}) copy-start(f32[4,256]{1,0:T(4,128)} %param.21) | copy-start | bytes 12292
  174.1 0.7 copy-start.1
  174.1 0.8 copy-start.3
  174.8 7.4 %copy-start.9 = (bf16[384,256]{1,0:T(8,128)(2,1)S(1)}, bf16[384,256]{1,0:T(8,128)(2,1)}, u32[]{:S(2)}) copy-start(bf16[384,256]{1,0:T(8,128)(2,1)} %param.17) | copy-start | bytes 589828
  174.8 389.6 %all-gather.7.cloned.1.call-start = ((), (), s32[]{:S(2)}) async-start(), calls=%async_computation.3 | async-start | bytes 17039360 | tf_op jit(solution)/shard_map/all_gather | solution.py:23
  175.6 536.8 %reduce-scatter.2.cloned.1.call-start = ((), (), s32[]{:S(2)}) async-start(), calls=%async_computation.1 | async-start | bytes 1769472 | tf_op jit(solution)/shard_map/reduce_scatter | solution.py:174
  176.3 5.9 collective-permute-start
  182.6 0.9 copy-start.4
  577.7 3.5 copy-start.5
  577.7 3.5 copy-start.6
  581.2 1.6 copy-start.7
  584.7 1.5 copy-start.11
Sparse Core Ops, SparseCore 0:
  174.9 196.4 all-gather.4
  374.4 190.0 all-gather.6
  590.0 122.3 reduce-scatter.1
where the time goes:
time: 722 us; the launch traced here: 719 us
  waiting for transfers between devices  502 us (70%)
  other arithmetic  127 us (18%)
  matrix products  46.4 us (6%)
  local copies, waits for them, and re-layouts  17.7 us (2%)
  between operations  13.5 us (2%)
  starting transfers between devices  11.7 us (2%)
    all_gather x2, waiting for transfers between devices, carried_in(): gathered = jax.tree.map(lambda a: lax.all_gather(a, axis), part)  379 us
    reduce_scatter x1, waiting for transfers between devices, shards(): lax.psum_scatter(jnp.dot(normed, out_weight, preferred_element_type=jnp.f...  123 us
    another operation x2, other arithmetic, block_parts(): lax.linalg.triangular_solve(system, rhs_both, left_side=True, lower=True,...  119 us
    dot_general x18, matrix products, stack_mul(): return jnp.einsum('bkl,blv->bkv', left, right, precision=PRECISE)  25.2 us
  transfers between devices with their start and end apart: 6, of which 3 were waited for; matrix products, arithmetic and copies ran while one was open for 19% of the time, Pallas kernels for 0%

commit v1 on v0

v1 whole, which is shorter than its diff:
```python
import functools
import jax, jax.numpy as jnp
from jax import lax
from jax.experimental import pallas as pl
from jax.experimental.pallas import tpu as pltpu
EPS=1e-6
F32=jnp.float32; BF=jnp.bfloat16
C=128
NC=3
def bdot(a,b):
    return lax.dot_general(a.astype(BF),b.astype(BF),(((1,),(0,)),((),())),preferred_element_type=F32)
def bdot_nt(a,b):
    return lax.dot_general(a.astype(BF),b.astype(BF),(((1,),(1,)),((),())),preferred_element_type=F32)
def split2(a):
    hi=a.astype(BF); lo=(a-hi.astype(F32)).astype(BF); return hi,lo
def dot3(a,b):
    ah,al=split2(a); bh,bl=split2(b)
    return bdot(ah,bh)+bdot(ah,bl)+bdot(al,bh)
def silu(x):
    return x/(1.0+jnp.exp(-x))
def softplus_of(x):
    e=jnp.exp(-jnp.abs(x)); u=1.0+e
    l=jnp.where(u==1.0,e,jnp.log(u)*e/jnp.where(u==1.0,1.0,u-1.0))
    return jnp.maximum(x,0.0)+l

def local_kernel(q_ref,k_ref,v_ref,halo_ref,qt_ref,kt_ref,vt_ref,bl_ref,dl_ref,
                 oloc_ref,qeff_ref,pair_ref,ext, *, prec=1):
    T=q_ref.shape[0]
    qc=q_ref.shape[1]; kc=k_ref.shape[1]; vc=v_ref.shape[1]
    ext[5:8,:]=halo_ref[...].astype(F32)
    ext[8:8+T,0:qc]=q_ref[...].astype(F32)
    ext[8:8+T,qc:qc+kc]=k_ref[...].astype(F32)
    ext[8:8+T,qc+kc:]=v_ref[...].astype(F32)
    def conv(lo,w_ref,wlo):
        s=w_ref[0:1,wlo:wlo+C]*ext[5:5+T,lo:lo+C]
        for j in range(1,4):
            s=s+w_ref[j:j+1,wlo:wlo+C]*ext[5+j:5+j+T,lo:lo+C]
        return silu(s)
    HKl=kc//C; HVl=vc//C; rep=HVl//HKl
    row=lax.broadcasted_iota(jnp.int32,(T,T),0); col=lax.broadcasted_iota(jnp.int32,(T,T),1)
    tri=(row>=col).astype(BF)
    beta=1.0/(1.0+jnp.exp(-bl_ref[...]))
    dec=-softplus_of(dl_ref[...])
    d1=dec.astype(BF); r=dec-d1.astype(F32); d2=r.astype(BF); d3=(r-d2.astype(F32)).astype(BF)
    lf=bdot(tri,d1)+bdot(tri,d2)+bdot(tri,d3)
    lfr=jnp.transpose(lf)
    ex=jnp.exp(lf)
    last=lf[T-1:T,:]
    tail=jnp.exp(last-lf)
    f1=jnp.exp(last)-1.0
    ri=lax.broadcasted_iota(jnp.int32,(C,C),0); ci=lax.broadcasted_iota(jnp.int32,(C,C),1)
    eye=(ri==ci).astype(F32)
    strict=ri>ci; within=ri>=ci
    sl=lambda c: slice(c*C,(c+1)*C)
    qs=[];ks=[];KK=[];QK=[];kT=[]
    for j in range(HKl):
        k=conv(qc+j*C,kt_ref,j*C)
        k=k*lax.rsqrt(jnp.sum(k*k,-1,keepdims=True)+EPS)
        q=conv(j*C,qt_ref,j*C)
        kb=k.astype(BF); qb=q.astype(BF)
        ks.append(kb); qs.append(qb)
        kT.append(jnp.transpose(k).astype(BF))
        KK.append({(c,e):bdot_nt(kb[sl(c)],kb[sl(e)]) for c in range(NC) for e in range(c+1)})
        QK.append({(c,e):bdot_nt(qb[sl(c)],kb[sl(e)]) for c in range(NC) for e in range(c+1)})
    A={};S={}
    for h in range(HVl):
        j=h//rep
        for c in range(NC):
            for e in range(c+1):
                g=jnp.exp(jnp.minimum(lf[sl(c),h:h+1]-lfr[h:h+1,sl(e)],0.0))
                s=g*QK[j][c,e]; a=(beta[sl(c),h:h+1]*g)*KK[j][c,e]
                if c==e:
                    s=jnp.where(within,s,0.0); a=jnp.where(strict,a,0.0)
                S[h,c,e]=s.astype(BF); A[h,c,e]=a
    keys=[(h,c) for h in range(HVl) for c in range(NC)]
    Tm={}
    def mask(s):
        return ((ri//(2*s))==(ci//(2*s)))&((ri//s)%2==1)&((ci//s)%2==0)
    m=mask(1)
    for key in keys:
        Tm[key]=eye-jnp.where(m,A[key+(key[1],)],0.0)
    s=2
    dd=bdot if prec==1 else dot3
    while s<C:
        m=mask(s)
        tmp={key:dd(jnp.where(m,A[key+(key[1],)],0.0),Tm[key]) for key in keys}
        Tm={key:Tm[key]-dd(Tm[key],tmp[key]) for key in keys}
        s*=2
    X={}
    for c in range(NC):
        for h in range(HVl):
            j=h//rep
            bcol=beta[sl(c),h:h+1]
            v=conv(qc+kc+h*C,vt_ref,h*C)[sl(c)] if False else None
        rhs={}
        for h in range(HVl):
            j=h//rep
            bcol=beta[sl(c),h:h+1]
            rr=ext_v(ext,vt_ref,qc+kc+h*C,h*C,c)
            R=jnp.concatenate([bcol*rr,(bcol*ex[sl(c),h:h+1])*ks[j][sl(c)].astype(F32)],1)
            for e in range(c):
                R=R-bdot(A[h,c,e],X[h,e])
            rhs[h]=R
        for h in range(HVl):
            X[h,c]=bdot(Tm[h,c],rhs[h])
    for h in range(HVl):
        j=h//rep
        for c in range(NC):
            ow=bdot(S[h,c,0],X[h,0])
            for e in range(1,c+1):
                ow=ow+bdot(S[h,c,e],X[h,e])
            oloc_ref[h,sl(c),:]=ow[:,:C]
            qeff_ref[h,sl(c),:]=(ex[sl(c),h:h+1]*qs[j][sl(c)].astype(F32)-ow[:,C:]).astype(BF)
        hw=None
        for c in range(NC):
            p=bdot(kT[j][:,sl(c)],tail[sl(c),h:h+1]*X[h,c])
            hw=p if hw is None else hw+p
        pair_ref[h,:,:C]=(f1[:,h:h+1]*eye-hw[:,C:]).astype(BF)
        pair_ref[h,:,C:]=hw[:,:C].astype(BF)
def ext_v(ext,w_ref,lo,wlo,c):
    s=w_ref[0:1,wlo:wlo+C]*ext[5+c*C:5+c*C+C,lo:lo+C]
    for j in range(1,4):
        s=s+w_ref[j:j+1,wlo:wlo+C]*ext[5+j+c*C:5+j+c*C+C,lo:lo+C]
    return silu(s)

def local_call(q,k,v,halo,qt,kt,vt,bl,dl,interpret=False,prec=1):
    T=q.shape[0]; HV=v.shape[1]//C
    return pl.pallas_call(functools.partial(local_kernel,prec=prec),
        out_shape=(jax.ShapeDtypeStruct((HV,T,C),F32),jax.ShapeDtypeStruct((HV,T,C),BF),jax.ShapeDtypeStruct((HV,C,2*C),BF)),
        scratch_shapes=[pltpu.VMEM((T+8,q.shape[1]+k.shape[1]+v.shape[1]),F32)],
        compiler_params=pltpu.CompilerParams(vmem_limit_bytes=48<<20),
        interpret=interpret)(q,k,v,halo,qt,kt,vt,bl,dl)

from jax.sharding import PartitionSpec as P
def comp(p2,p1):
    return p2+p1+jnp.einsum("hij,hjk->hik",p2[...,:C].astype(BF),p1.astype(BF),preferred_element_type=F32)
def app(p,s):
    return s+p[...,C:]+jnp.einsum("hij,hjk->hik",p[...,:C].astype(BF),s.astype(BF),preferred_element_type=F32)

def finish_kernel(oloc_ref,qeff_ref,sin_ref,gate_ref,gain_ref,w_ref,out_ref,nrm):
    for h in range(oloc_ref.shape[0]):
        o=oloc_ref[h]+bdot(qeff_ref[h],sin_ref[h])
        o=o*lax.rsqrt(jnp.mean(o*o,-1,keepdims=True)+EPS)
        o=o*gain_ref[...]*silu(gate_ref[:,h*C:(h+1)*C].astype(F32))
        nrm[:,h*C:(h+1)*C]=o.astype(BF)
    for n in range(0,w_ref.shape[1],512):
        out_ref[:,n:n+512]=bdot(nrm[...],w_ref[:,n:n+512]).astype(BF)

def shards(q,k,v,gate,qt,kt,vt,bl,dl,gain,w):
    tail=jnp.concatenate([q[-3:],k[-3:],v[-3:]],1)
    n=lax.axis_size("seq")
    halo=lax.ppermute(tail,"seq",[(i,i+1) for i in range(n-1)])
    oloc,qeff,pair=local_call(q,k,v,halo,qt,kt,vt,bl,dl)
    me=lax.axis_index("seq"); x=me//16; z=me%16
    allp=lax.all_gather(pair,"seq",axis_index_groups=[[16*i+j for j in range(16)] for i in range(4)])
    zero=jnp.zeros(pair.shape,F32)
    def one(i,c):
        acc,pre=c
        pre=jnp.where(i==z,acc,pre)
        return comp(lax.dynamic_index_in_dim(allp,i,0,False).astype(F32),acc),pre
    tot,pre=lax.fori_loop(0,16,one,(zero,zero))
    rows=lax.all_gather(tot.astype(BF),"seq",axis_index_groups=[[16*i+j for i in range(4)] for j in range(16)])
    s=jnp.zeros((pair.shape[0],C,C),F32); mine=s
    for i in range(4):
        mine=jnp.where(i==x,s,mine)
        s=app(rows[i].astype(F32),s)
    sin=app(pre,mine).astype(BF)
    part=pl.pallas_call(finish_kernel,out_shape=jax.ShapeDtypeStruct((q.shape[0],w.shape[1]),BF),
        scratch_shapes=[pltpu.VMEM((q.shape[0],w.shape[0]),BF)],
        compiler_params=pltpu.CompilerParams(vmem_limit_bytes=48<<20))(oloc,qeff,sin,gate,gain.reshape(1,C),w)
    return lax.psum_scatter(part,"head",scatter_dimension=0,tiled=True)

def solution(mesh):
    placed=(P("seq","head"),)*4+(P(None,"head"),)*3+(P("seq","head"),)*2+(P(),P("head",None))
    return jax.shard_map(shards,mesh=mesh,in_specs=placed,out_specs=P(("seq","head"),None),check_vma=False)
```

time: 722 us -> 277 us (0.38)
  waiting for transfers between devices: 502 us -> 152 us
  other arithmetic: 127 us -> 31.7 us
  matrix products: 46.4 us -> 20.9 us
  local copies, waits for them, and re-layouts: 17.7 us -> 42.6 us
  Pallas kernels: 0 us -> 8.63 us
  starting transfers between devices: 11.7 us -> 4.46 us
    all_gather x2, waiting for transfers between devices: 379 us -> 112 us  [the longest x1 76 us: shards(): lax.all_gather(pair, 'seq', axis_index_groups=[[16 * i + j for j in range...]
    another operation x3 -> x0, other arithmetic: 120 us -> none  [the longest x2 119 us: block_parts(): lax.linalg.triangular_solve(system, rhs_both, left_side=True, lower=True,...]
    reduce_scatter x1, waiting for transfers between devices: 123 us -> 40.1 us  [shards(): return lax.psum_scatter(part, 'head', scatter_dimension=0, tiled=True)]
    select_n x0 -> x16, other arithmetic: none -> 29.7 us  [one(): pre = jnp.where(i == z, acc, pre)]
    dot_general x26 -> x20, matrix products: 44.8 us -> 20.9 us  [the longest x16 16.3 us: comp(): jnp.einsum('hij,hjk->hik', p2[..., :C].astype(BF), p1.astype(BF), preferr...]
    while x18 -> x16, local copies, waits for them, and re-layouts: 0.34 us -> 16.7 us
    convert_element_type x1 -> x16, local copies, waits for them, and re-layouts: 2.07 us -> 15.5 us  [one(): lax.dynamic_index_in_dim(allp, i, 0, False).astype(F32)]
    pallas_call x0 -> x2, Pallas kernels: none -> 8.63 us  [the longest x1 6 us: local_call(): pl.pallas_call(functools.partial(local_kernel, prec=prec), out_shape=(jax...]
  transfers between devices with their start and end apart: 6 -> 4, of which waited for: 3 -> 3; matrix products, arithmetic and copies ran while one was open for 19% -> 1% of each run, Pallas kernels for 0% -> 0%
where the time goes in v1:
time: 277 us; the launch traced here: 274 us
  waiting for transfers between devices  152 us (55%)
  local copies, waits for them, and re-layouts  42.6 us (15%)
  other arithmetic  31.7 us (11%)
  matrix products  20.9 us (8%)
  between operations  13.3 us (5%)
  Pallas kernels  8.63 us (3%)
  starting transfers between devices  4.46 us (2%)
    all_gather x1, waiting for transfers between devices, shards(): lax.all_gather(pair, 'seq', axis_index_groups=[[16 * i + j for j in range...  76 us
    reduce_scatter x1, waiting for transfers between devices, shards(): return lax.psum_scatter(part, 'head', scatter_dimension=0, tiled=True)  40.1 us
    all_gather x1, waiting for transfers between devices, shards(): lax.all_gather(tot.astype(BF), 'seq', axis_index_groups=[[16 * i + j for...  36.2 us
    select_n x16, other arithmetic, one(): pre = jnp.where(i == z, acc, pre)  29.7 us
    while x16, local copies, waits for them, and re-layouts  16.7 us
    dot_general x16, matrix products, comp(): jnp.einsum('hij,hjk->hik', p2[..., :C].astype(BF), p1.astype(BF), preferr...  16.3 us
    convert_element_type x16, local copies, waits for them, and re-layouts, one(): lax.dynamic_index_in_dim(allp, i, 0, False).astype(F32)  15.5 us
    unnamed x24, local copies, waits for them, and re-layouts  8.34 us
  transfers between devices with their start and end apart: 4, of which 3 were waited for; matrix products, arithmetic and copies ran while one was open for 1% of the time, Pallas kernels for 0%

profile of v1, /device:TPU:1, one launch (start us, length us, event | category | flops | bytes accessed | tf_op | source)
XLA Modules:
  0.0 273.9 jit_solution(10016372440468685507)
XLA Ops:
  8.6 4.4 %collective-permute-start = (bf16[3,1024]{1,0:T(4,128)(2,1)S(1)}, bf16[3,1024]{1,0:T(4,128)(2,1)S(1)}, u32[]{:S(2)}, u32[]{:S(2)}) collective-permute-start(bf16[3,1024]{1,0:T(4,128)(2,1)S(1)} %pad_maximum_fusion), channel_id=1, source_target_pairs={{0,8},{8,16},{16,24},{24,32},{32,40},{40,48},{48,56},{56,64},{64,7... | collective-permute-start | bytes 18440 | tf_op jit(solution)/shard_map/ppermute | solution.py:152
  19.6 6.0 %shard_map.109 = (f32[4,384,128]{2,1,0:T(8,128)S(1)}, bf16[4,384,128]{2,1,0:T(8,128)(2,1)S(1)}, bf16[4,128,256]{2,1,0:T(8,128)(2,1)}) custom-call(bf16[384,256]{1,0:T(8,128)(2,1)S(1)} %copy-done.5, bf16[384,256]{1,0:T(8,128)(2,1)S(1)} %copy-done.6, bf16[384,512]{1,0:T(8,128)(2,1)S(1)} %copy-done.1, bf16[3,1024]{1,0:T(4,128)(2,1)S(1)} %collective-permute-done.halo_ref, ...), custom_call_target="tpu_custom_call" | custom-call | tf_op jit(solution)/shard_map/pallas_call | solution.py:128
  26.5 76.0 %all-gather.5.cloned.1.call-done = bf16[64,128,256]{2,1,0:T(8,128)(2,1)} async-done(((bf16[4,128,256]{2,1,0:T(8,128)(2,1)}), bf16[64,128,256]{2,1,0:T(8,128)(2,1)}) %all-gather.5.cloned.1.call-update) | async-done | bytes 4194320 | tf_op jit(solution)/shard_map/all_gather | solution.py:155
  102.5 78.2 %while.16 = (s32[]{:T(128)}, f32[4,128,256]{2,1,0:T(8,128)}, f32[4,128,256]{2,1,0:T(8,128)}, bf16[16,4,128,256]{3,2,1,0:T(8,128)(2,1)}, s32[]{:T(128)}, /*index=5*/s32[]{:T(128)}, s32[]{:T(128)}) while((s32[]{:T(128)}, f32[4,128,256]{2,1,0:T(8,128)}, f32[4,128,256]{2,1,0:T(8,128)}, bf16[16,4,128,256]{3,2,1,0:T(8,128)(2,1)}, ...), condition=%wide.region_1.2_spmd.clone, body=%wide.region_0.1_spmd.clone.sunk | while | flops 34734080 | bytes 5112941 | solution.py:161
  108.5 1.9 select_select_fusion.2
  113.4 1.9 select_select_fusion.2
  118.4 1.9 select_select_fusion.2
  123.3 1.9 select_select_fusion.2
  128.3 1.9 select_select_fusion.2
  133.2 1.9 select_select_fusion.2
  138.2 1.9 select_select_fusion.2
  143.1 1.9 select_select_fusion.2
  148.1 1.9 select_select_fusion.2
  153.0 1.9 select_select_fusion.2
  158.0 1.9 select_select_fusion.2
  162.9 1.9 select_select_fusion.2
  167.9 1.9 select_select_fusion.2
  172.8 1.9 select_select_fusion.2
  177.8 1.9 select_select_fusion.2
  180.7 1.9 convert_element_type.56
  182.8 36.2 %all-gather.7.cloned.1.call-done = bf16[16,128,256]{2,1,0:T(8,128)(2,1)} async-done(((bf16[4,128,256]{2,1,0:T(8,128)(2,1)}), bf16[16,128,256]{2,1,0:T(8,128)(2,1)}) %all-gather.7.cloned.1.call-update) | async-done | bytes 1048592 | tf_op jit(solution)/shard_map/all_gather | solution.py:162
  222.4 1.2 fusion.5.sin_ref
  224.6 2.6 shard_map.110
  227.2 40.1 %reduce-scatter.2.cloned.1.call-done = bf16[48,2048]{1,0:T(8,128)(2,1)} async-done(((bf16[384,2048]{1,0:T(8,128)(2,1)}), bf16[48,2048]{1,0:T(8,128)(2,1)}) %reduce-scatter.2.cloned.1.call-update) | async-done | bytes 196624 | tf_op jit(solution)/shard_map/reduce_scatter | solution.py:171
  (89 shorter events, 63.3 us)
Async XLA Ops:
  6.5 96.0 %all-gather.5.cloned.1.call-start = ((), (), s32[]{:S(2)}) async-start(), calls=%async_computation.2 | async-start | bytes 4456448 | tf_op jit(solution)/shard_map/all_gather | solution.py:155
  8.6 6.0 %collective-permute-start = (bf16[3,1024]{1,0:T(4,128)(2,1)S(1)}, bf16[3,1024]{1,0:T(4,128)(2,1)S(1)}, u32[]{:S(2)}, u32[]{:S(2)}) collective-permute-start(bf16[3,1024]{1,0:T(4,128)(2,1)S(1)} %pad_maximum_fusion), channel_id=1, source_target_pairs={{0,8},{8,16},{16,24},{24,32},{32,40},{40,48},{48,56},{56,64},{64,7... | collective-permute-start | bytes 18440 | tf_op jit(solution)/shard_map/ppermute | solution.py:152
  14.7 1.0 copy-start.1
  15.7 0.9 copy-start.5
  16.6 0.9 copy-start.6
  17.5 0.7 copy-start.7
  18.2 0.7 copy-start.8
  18.9 0.7 copy-start.9
  25.6 0.8 copy-start.3
  26.4 192.5 %all-gather.7.cloned.1.call-start = ((), (), s32[]{:S(2)}) async-start(), calls=%async_computation.3 | async-start | bytes 1310720 | tf_op jit(solution)/shard_map/all_gather | solution.py:162
  102.5 121.1 %copy-start.2 = (bf16[384,512]{1,0:T(8,128)(2,1)S(1)}, bf16[384,512]{1,0:T(8,128)(2,1)}, u32[]{:S(2)}) copy-start(bf16[384,512]{1,0:T(8,128)(2,1)} %gate_ref.1) | copy-start | bytes 1179652
  102.5 121.1 %copy-start.10 = (f32[128]{0:T(128)S(1)}, f32[128]{0:T(128)}, u32[]{:S(2)}) copy-start(f32[128]{0:T(128)} %param.22) | copy-start | bytes 1540
  180.7 42.9 %copy-start = (bf16[512,2048]{1,0:T(8,128)(2,1)S(1)}, bf16[512,2048]{1,0:T(8,128)(2,1)}, u32[]{:S(2)}) copy-start(bf16[512,2048]{1,0:T(8,128)(2,1)} %w_ref.1) | copy-start | bytes 6291460
  182.7 84.6 %reduce-scatter.2.cloned.1.call-start = ((), (), s32[]{:S(2)}) async-start(), calls=%async_computation.1 | async-start | bytes 1769472 | tf_op jit(solution)/shard_map/reduce_scatter | solution.py:171
  223.6 1.0 copy-start.4
Sparse Core Ops, SparseCore 0:
  26.5 75.9 all-gather.4
  182.8 36.0 all-gather.6
  227.4 39.9 reduce-scatter.1

commit v2 on v1

--- a/solution.py
+++ b/solution.py
@@ -128,47 +128,176 @@
     return pl.pallas_call(functools.partial(local_kernel,prec=prec),
         out_shape=(jax.ShapeDtypeStruct((HV,T,C),F32),jax.ShapeDtypeStruct((HV,T,C),BF),jax.ShapeDtypeStruct((HV,C,2*C),BF)),
         scratch_shapes=[pltpu.VMEM((T+8,q.shape[1]+k.shape[1]+v.shape[1]),F32)],
-        compiler_params=pltpu.CompilerParams(vmem_limit_bytes=48<<20),
+        compiler_params=pltpu.CompilerParams(vmem_limit_bytes=60<<20),
         interpret=interpret)(q,k,v,halo,qt,kt,vt,bl,dl)
 
 from jax.sharding import PartitionSpec as P
-def comp(p2,p1):
-    return p2+p1+jnp.einsum("hij,hjk->hik",p2[...,:C].astype(BF),p1.astype(BF),preferred_element_type=F32)
-def app(p,s):
-    return s+p[...,C:]+jnp.einsum("hij,hjk->hik",p[...,:C].astype(BF),s.astype(BF),preferred_element_type=F32)
-
-def finish_kernel(oloc_ref,qeff_ref,sin_ref,gate_ref,gain_ref,w_ref,out_ref,nrm):
-    for h in range(oloc_ref.shape[0]):
-        o=oloc_ref[h]+bdot(qeff_ref[h],sin_ref[h])
+MESH=pl.DeviceIdType.MESH
+NL=4
+NG=4
+NX=4
+NY=4
+CH=4
+
+def compose(later,earlier):
+    return later+earlier+bdot(later[:,:C],earlier)
+
+def exchange(axis,me_slot,device_of,src_of,land,send,recv):
+    copies=[]
+    for off in range(1,4):
+        slot=lax.rem(me_slot+off,4)
+        cp=pltpu.make_async_remote_copy(src_ref=src_of(slot),dst_ref=land.at[me_slot],send_sem=send.at[off-1],
+            recv_sem=recv.at[me_slot],device_id={axis:device_of(slot)},device_id_type=MESH)
+        cp.start()
+        copies.append(cp)
+    def finish():
+        for off in range(1,4):
+            slot=lax.rem(me_slot+off,4)
+            pltpu.make_async_remote_copy(src_ref=src_of(slot),dst_ref=land.at[slot],send_sem=send.at[off-1],
+                recv_sem=recv.at[slot],device_id={axis:device_of(slot)},device_id_type=MESH).wait_recv()
+    return copies,finish
+
+def scan_body(pair,sin,buf1,pre,tot,buf2,gpre,rowt,buf3,rpre,outb,s1,r1,s2,r2,s3,r3,s4,r4):
+    me=lax.axis_index("seq")
+    l=lax.rem(me,NL); g=lax.rem(me//NL,NG); x=me//(NL*NG)
+    dl=lambda i: me-l+i
+    dg=lambda i: me+(i-g)*NL
+    dx=lambda i: me+(i-x)*(NL*NG)
+    c1,w1=exchange("seq",l,dl,lambda i: pair.at[i],buf1,s1,r1)
+    buf1[l]=pair[l]
+    w1()
+    acc=buf1[0].astype(F32)
+    pre[0]=jnp.zeros((C,2*C),F32)
+    for i in range(1,NL):
+        pre[i]=acc
+        acc=compose(buf1[i].astype(F32),acc)
+    tot[...]=acc.astype(BF)
+    c2,w2=exchange("seq",g,dg,lambda i: tot,buf2,s2,r2)
+    buf2[g]=tot[...]
+    w2()
+    acc=buf2[0].astype(F32)
+    gpre[0]=jnp.zeros((C,2*C),F32)
+    for i in range(1,NG):
+        gpre[i]=acc
+        acc=compose(buf2[i].astype(F32),acc)
+    rowt[...]=acc.astype(BF)
+    c3,w3=exchange("seq",x,dx,lambda i: rowt,buf3,s3,r3)
+    buf3[x]=rowt[...]
+    w3()
+    s=buf3[0,:,C:].astype(F32)
+    rpre[0]=jnp.zeros((C,C),F32)
+    for i in range(1,NX):
+        rpre[i]=s
+        s=s+buf3[i,:,C:].astype(F32)+bdot(buf3[i,:,:C],s)
+    row_in=rpre[x]
+    gp=gpre[g]
+    grp=row_in+gp[:,C:]+bdot(gp[:,:C],row_in)
+    for i in range(NL):
+        p=pre[i]
+        outb[i]=(grp+p[:,C:]+bdot(p[:,:C],grp)).astype(BF)
+    c4,w4=exchange("seq",l,dl,lambda i: outb.at[i],sin,s4,r4)
+    sin[l]=outb[l]
+    w4()
+    for cp in c1+c2+c3+c4:
+        cp.wait_send()
+
+def scan_peers():
+    me=lax.axis_index("seq")
+    l=lax.rem(me,NL); g=lax.rem(me//NL,NG); x=me//(NL*NG)
+    out=[]
+    for off in range(1,4):
+        out.append(me-l+lax.rem(l+off,4))
+        out.append(me+(lax.rem(g+off,4)-g)*NL)
+        out.append(me+(lax.rem(x+off,4)-x)*(NL*NG))
+    return out
+
+def scan_kernel(pair,out,sin,*rest):
+    barrier=pltpu.get_barrier_semaphore()
+    for d in scan_peers():
+        pl.semaphore_signal(barrier,inc=1,device_id={"seq":d},device_id_type=MESH)
+    pl.semaphore_wait(barrier,9)
+    scan_body(pair,sin,*rest)
+    out[...]=sin[...]
+
+def scan_scratch():
+    D=pltpu.SemaphoreType.DMA
+    return [pltpu.VMEM((4,C,C),BF),pltpu.VMEM((4,C,2*C),BF),pltpu.VMEM((4,C,2*C),F32),pltpu.VMEM((C,2*C),BF),
+        pltpu.VMEM((4,C,2*C),BF),pltpu.VMEM((4,C,2*C),F32),pltpu.VMEM((C,2*C),BF),pltpu.VMEM((4,C,2*C),BF),
+        pltpu.VMEM((4,C,C),F32),pltpu.VMEM((4,C,C),BF)]+[D((3,)),D((4,))]*4
+
+def scan_call(pair):
+    return pl.pallas_call(scan_kernel,out_shape=jax.ShapeDtypeStruct((4,C,C),BF),scratch_shapes=scan_scratch(),
+        compiler_params=pltpu.CompilerParams(collective_id=1,has_side_effects=True,vmem_limit_bytes=60<<20))(pair)
+
+def finish_body(oloc,qeff,sin,gate,gain,w,out,nrm,part,land,pair_sum,gath,sa,ra,sb,rb):
+    hd=lax.axis_index("head"); y=hd//2; c=lax.rem(hd,2)
+    for h in range(4):
+        o=oloc[h]+bdot(qeff[h],sin[h])
         o=o*lax.rsqrt(jnp.mean(o*o,-1,keepdims=True)+EPS)
-        o=o*gain_ref[...]*silu(gate_ref[:,h*C:(h+1)*C].astype(F32))
+        o=o*gain[...]*silu(gate[:,h*C:(h+1)*C].astype(F32))
         nrm[:,h*C:(h+1)*C]=o.astype(BF)
-    for n in range(0,w_ref.shape[1],512):
-        out_ref[:,n:n+512]=bdot(nrm[...],w_ref[:,n:n+512]).astype(BF)
+    wide=w.shape[1]//CH
+    rows=nrm.shape[0]//8
+    def first(n):
+        return pltpu.make_async_remote_copy(src_ref=part.at[n,1-c],dst_ref=land.at[n],send_sem=sa.at[n],recv_sem=ra.at[n],
+            device_id={"head":hd+1-2*c},device_id_type=MESH)
+    for n in range(CH):
+        p=bdot(nrm[...],w[:,n*wide:(n+1)*wide]).astype(BF)
+        for b in range(8):
+            part[n,b%2,b//2]=p[b*rows:(b+1)*rows]
+        first(n).start()
+    def second(n,off,slot):
+        to=lax.rem(y+off,NY)
+        return pltpu.make_async_remote_copy(src_ref=pair_sum.at[n,to],dst_ref=gath.at[n,slot],send_sem=sb.at[n,off-1],
+            recv_sem=rb.at[n,slot],device_id={"head":2*to+c},device_id_type=MESH)
+    for n in range(CH):
+        first(n).wait_recv()
+        pair_sum[n]=(part[n,c].astype(F32)+land[n].astype(F32)).astype(BF)
+        for off in range(1,4):
+            second(n,off,y).start()
+        gath[n,y]=pair_sum[n,y]
+    for n in range(CH):
+        for off in range(1,4):
+            second(n,off,lax.rem(y+off,NY)).wait_recv()
+        t=gath[n,0].astype(F32)
+        for i in range(1,NY):
+            t=t+gath[n,i].astype(F32)
+        out[:,n*wide:(n+1)*wide]=t.astype(BF)
+    for n in range(CH):
+        first(n).wait_send()
+        for off in range(1,4):
+            second(n,off,y).wait_send()
+
+def finish_peers():
+    hd=lax.axis_index("head"); y=hd//2; c=lax.rem(hd,2)
+    return [hd+1-2*c]+[2*lax.rem(y+off,NY)+c for off in range(1,4)]
+
+def finish_kernel(*refs):
+    barrier=pltpu.get_barrier_semaphore()
+    for d in finish_peers():
+        pl.semaphore_signal(barrier,inc=1,device_id={"head":d},device_id_type=MESH)
+    pl.semaphore_wait(barrier,4)
+    finish_body(*refs)
+
+def finish_scratch(T,K,N):
+    D=pltpu.SemaphoreType.DMA
+    r=T//8; wide=N//CH
+    return [pltpu.VMEM((T,K),BF),pltpu.VMEM((CH,2,4,r,wide),BF),pltpu.VMEM((CH,4,r,wide),BF),pltpu.VMEM((CH,4,r,wide),BF),
+        pltpu.VMEM((CH,4,r,wide),BF),D((CH,)),D((CH,)),D((CH,3)),D((CH,4))]
+
+def finish_call(oloc,qeff,sin,gate,gain,w):
+    T=gate.shape[0]
+    return pl.pallas_call(finish_kernel,out_shape=jax.ShapeDtypeStruct((T//8,w.shape[1]),BF),
+        scratch_shapes=finish_scratch(T,w.shape[0],w.shape[1]),
+        compiler_params=pltpu.CompilerParams(collective_id=2,has_side_effects=True,vmem_limit_bytes=60<<20))(oloc,qeff,sin,gate,gain,w)
 
 def shards(q,k,v,gate,qt,kt,vt,bl,dl,gain,w):
     tail=jnp.concatenate([q[-3:],k[-3:],v[-3:]],1)
     n=lax.axis_size("seq")
     halo=lax.ppermute(tail,"seq",[(i,i+1) for i in range(n-1)])
     oloc,qeff,pair=local_call(q,k,v,halo,qt,kt,vt,bl,dl)
-    me=lax.axis_index("seq"); x=me//16; z=me%16
-    allp=lax.all_gather(pair,"seq",axis_index_groups=[[16*i+j for j in range(16)] for i in range(4)])
-    zero=jnp.zeros(pair.shape,F32)
-    def one(i,c):
-        acc,pre=c
-        pre=jnp.where(i==z,acc,pre)
-        return comp(lax.dynamic_index_in_dim(allp,i,0,False).astype(F32),acc),pre
-    tot,pre=lax.fori_loop(0,16,one,(zero,zero))
-    rows=lax.all_gather(tot.astype(BF),"seq",axis_index_groups=[[16*i+j for i in range(4)] for j in range(16)])
-    s=jnp.zeros((pair.shape[0],C,C),F32); mine=s
-    for i in range(4):
-        mine=jnp.where(i==x,s,mine)
-        s=app(rows[i].astype(F32),s)
-    sin=app(pre,mine).astype(BF)
-    part=pl.pallas_call(finish_kernel,out_shape=jax.ShapeDtypeStruct((q.shape[0],w.shape[1]),BF),
-        scratch_shapes=[pltpu.VMEM((q.shape[0],w.shape[0]),BF)],
-        compiler_params=pltpu.CompilerParams(vmem_limit_bytes=48<<20))(oloc,qeff,sin,gate,gain.reshape(1,C),w)
-    return lax.psum_scatter(part,"head",scatter_dimension=0,tiled=True)
+    sin=scan_call(pair)
+    return finish_call(oloc,qeff,sin,gate,gain.reshape(1,C),w)
 
 def solution(mesh):
     placed=(P("seq","head"),)*4+(P(None,"head"),)*3+(P("seq","head"),)*2+(P(),P("head",None))

time: 277 us -> 87.1 us (0.31)
  waiting for transfers between devices: 152 us -> 0.01 us
  Pallas kernels: 8.63 us -> 75 us
  local copies, waits for them, and re-layouts: 42.6 us -> 7.31 us
  other arithmetic: 31.7 us -> 0.01 us
  matrix products: 20.9 us -> 0 us
  between operations: 13.3 us -> 0.03 us
    all_gather x2 -> x0, waiting for transfers between devices: 112 us -> none  [the longest x1 76 us: shards(): lax.all_gather(pair, 'seq', axis_index_groups=[[16 * i + j for j in range...]
    pallas_call x1 -> x2, Pallas kernels: 2.63 us -> 67.1 us  [the longest x1 45.7 us: scan_call(): pl.pallas_call(scan_kernel, out_shape=jax.ShapeDtypeStruct((4, C, C), BF)...]
    reduce_scatter x1 -> x0, waiting for transfers between devices: 40.1 us -> none  [shards(): return lax.psum_scatter(part, 'head', scatter_dimension=0, tiled=True)]
    select_n x16 -> x0, other arithmetic: 29.7 us -> none  [one(): pre = jnp.where(i == z, acc, pre)]
    dot_general x20 -> x0, matrix products: 20.9 us -> none  [the longest x16 16.3 us: comp(): jnp.einsum('hij,hjk->hik', p2[..., :C].astype(BF), p1.astype(BF), preferr...]
    while x16 -> x0, local copies, waits for them, and re-layouts: 16.7 us -> none
    convert_element_type x16 -> x0, local copies, waits for them, and re-layouts: 15.5 us -> none  [one(): lax.dynamic_index_in_dim(allp, i, 0, False).astype(F32)]
    unnamed x24 -> x5, local copies, waits for them, and re-layouts: 8.34 us -> 5.22 us
  transfers between devices with their start and end apart: 4 -> 1, of which waited for: 3 -> 0; matrix products, arithmetic and copies ran while one was open for 1% -> 3% of each run, Pallas kernels for 0% -> 0%
where the time goes in v2:
time: 87.1 us; the launch traced here: 86.7 us
  Pallas kernels  75 us (86%)
  local copies, waits for them, and re-layouts  7.31 us (8%)
  starting transfers between devices  4.37 us (5%)
    pallas_call x1, Pallas kernels, scan_call(): pl.pallas_call(scan_kernel, out_shape=jax.ShapeDtypeStruct((4, C, C), BF)...  45.7 us
    pallas_call x1, Pallas kernels, finish_call(): pl.pallas_call(finish_kernel, out_shape=jax.ShapeDtypeStruct((T // 8, w.s...  21.4 us
    pallas_call x1, Pallas kernels, local_call(): pl.pallas_call(functools.partial(local_kernel, prec=prec), out_shape=(jax...  7.85 us
    unnamed x5, local copies, waits for them, and re-layouts  5.22 us
    ppermute x1, starting transfers between devices, shards(): halo = lax.ppermute(tail, 'seq', [(i, i + 1) for i in range(n - 1)])  4.37 us
    slice x3, local copies, waits for them, and re-layouts, shards(): tail = jnp.concatenate([q[-3:], k[-3:], v[-3:]], 1)  2.08 us
  transfers between devices with their start and end apart: 1, of which 0 were waited for; matrix products, arithmetic and copies ran while one was open for 3% of the time, Pallas kernels for 0%

profile of v2, /device:TPU:1, one launch (start us, length us, event | category | flops | bytes accessed | tf_op | source)
XLA Modules:
  0.0 86.7 jit_solution(1818172684239959060)
XLA Ops:
  0.0 0.7 slice.9
  0.7 0.7 slice.10
  1.4 0.7 slice.11
  2.1 4.4 %collective-permute-start = (bf16[3,1024]{1,0:T(4,128)(2,1)S(1)}, bf16[3,1024]{1,0:T(4,128)(2,1)S(1)}, u32[]{:S(2)}, u32[]{:S(2)}) collective-permute-start(bf16[3,1024]{1,0:T(4,128)(2,1)S(1)} %pad_maximum_fusion), channel_id=1, source_target_pairs={{0,8},{8,16},{16,24},{24,32},{32,40},{40,48},{48,56},{56,64},{64,7... | collective-permute-start | bytes 18440 | tf_op jit(solution)/shard_map/ppermute | solution.py:297
  6.5 1.5 %copy.12.bl_ref = f32[384,4]{1,0:T(8,128)} copy(f32[384,4]{0,1:T(4,128)} %param.18) | data formatting | bytes 12288 | tf_op args[7]
  8.0 1.5 %copy.13.dl_ref = f32[384,4]{1,0:T(8,128)} copy(f32[384,4]{0,1:T(4,128)} %param.19) | data formatting | bytes 12288 | tf_op args[8]
  9.5 0.0 collective-permute-done.halo_ref
  9.5 0.0 copy-start
  9.5 0.6 copy-done
  10.1 7.8 %shard_map.109 = (f32[4,384,128]{2,1,0:T(8,128)}, bf16[4,384,128]{2,1,0:T(8,128)(2,1)}, bf16[4,128,256]{2,1,0:T(8,128)(2,1)}) custom-call(bf16[384,256]{1,0:T(8,128)(2,1)} %q_ref.1, bf16[384,256]{1,0:T(8,128)(2,1)} %k_ref.1, bf16[384,512]{1,0:T(8,128)(2,1)} %v_ref.1, bf16[3,1024]{1,0:T(4,128)(2,1)} %copy-done, f32[4,256]{1,0:T(4,128)} %qt_ref.1, ...), custom_call_target="tpu_custom_call" | custom-call | tf_op jit(solution)/shard_map/pallas_call | solution.py:128
  17.9 45.7 %shard_map.110.refs_2_ = bf16[4,128,128]{2,1,0:T(8,128)(2,1)} custom-call(bf16[4,128,256]{2,1,0:T(8,128)(2,1)} %get-tuple-element.10.pair), custom_call_target="tpu_custom_call" | custom-call | tf_op jit(solution)/shard_map/pallas_call | solution.py:229
  63.7 21.4 %shard_map.111 = bf16[48,2048]{1,0:T(8,128)(2,1)} custom-call(f32[4,384,128]{2,1,0:T(8,128)} %get-tuple-element.8.refs_0_, bf16[4,384,128]{2,1,0:T(8,128)(2,1)} %get-tuple-element.9.refs_1_, bf16[4,128,128]{2,1,0:T(8,128)(2,1)} %shard_map.110.refs_2_, bf16[384,512]{1,0:T(8,128)(2,1)} %refs_3_.1, f32[1,128]{1,0:T(1,128)} %bitcast.1, bf16[512,2048]{1,0:T(8,128)(2,1)} %refs_5_.1), custom_call_target="tpu_custom_call" | custom-call | tf_op jit(solution)/shard_map/pallas_call | solution.py:290
  85.1 1.6 %copy.15 = bf16[48,2048]{1,0:T(8,128)(2,1)} copy(bf16[48,2048]{1,0:T(8,128)(2,1)} %shard_map.111) | data formatting | bytes 393216
  (1 shorter events, 0.0 us)
Async XLA Ops:
  2.1 7.4 %collective-permute-start = (bf16[3,1024]{1,0:T(4,128)(2,1)S(1)}, bf16[3,1024]{1,0:T(4,128)(2,1)S(1)}, u32[]{:S(2)}, u32[]{:S(2)}) collective-permute-start(bf16[3,1024]{1,0:T(4,128)(2,1)S(1)} %pad_maximum_fusion), channel_id=1, source_target_pairs={{0,8},{8,16},{16,24},{24,32},{32,40},{40,48},{48,56},{56,64},{64,7... | collective-permute-start | bytes 18440 | tf_op jit(solution)/shard_map/ppermute | solution.py:297
  9.5 0.6 copy-start

commit v3 on v0

v3 whole, which is shorter than its diff:
```python
import jax
import jax.numpy as jnp
from jax import lax
from jax.experimental import pallas as pl
from jax.experimental.pallas import tpu as pltpu
from jax.sharding import PartitionSpec as P

EPS = 1e-6
F32 = jnp.float32
BF = jnp.bfloat16
MESH = pl.DeviceIdType.MESH
C = 128
NL = 4
NG = 4
NX = 4
NY = 4
CH = 4
HALO = 16


def bdot(a, b):
    return lax.dot_general(
        a.astype(BF), b.astype(BF), (((1,), (0,)), ((), ())), preferred_element_type=F32
    )


def bdot_nt(a, b):
    return lax.dot_general(
        a.astype(BF), b.astype(BF), (((1,), (1,)), ((), ())), preferred_element_type=F32
    )


def silu(x):
    return x / (1.0 + jnp.exp(-x))


def softplus(x):
    e = jnp.exp(-jnp.abs(x))
    u = 1.0 + e
    log1p = jnp.where(u == 1.0, e, jnp.log(u) * e / jnp.where(u == 1.0, 1.0, u - 1.0))
    return jnp.maximum(x, 0.0) + log1p


def compose(later, earlier):
    return later + earlier + bdot(later[:, :C], earlier)


def applied(pair, state):
    return state + pair[:, C:] + bdot(pair[:, :C], state)


def place():
    me = lax.axis_index("seq")
    return me, lax.rem(me, NL), lax.rem(me // NL, NG), me // (NL * NG)


def signal_all(devices):
    barrier = pltpu.get_barrier_semaphore()
    for d in devices:
        pl.semaphore_signal(barrier, inc=1, device_id=d, device_id_type=MESH)


def wait_all(count):
    pl.semaphore_wait(pltpu.get_barrier_semaphore(), count)


def halo_kernel(q, k, v, out, land, send, recv):
    me = lax.axis_index("seq")
    n = lax.axis_size("seq")
    after = {"seq": lax.rem(me + 1, n)}
    before = {"seq": lax.rem(me + n - 1, n)}
    signal_all([after, before])
    wait_all(2)
    copies = []
    lo = 0
    for i, ref in enumerate((q, k, v)):
        t, w = ref.shape
        copies.append(
            pltpu.make_async_remote_copy(
                src_ref=ref.at[pl.ds(t - HALO, HALO)],
                dst_ref=land.at[:, pl.ds(lo, w)],
                send_sem=send.at[i],
                recv_sem=recv.at[i],
                device_id=after,
                device_id_type=MESH,
            )
        )
        copies[-1].start()
        lo += w
    for copy in copies:
        copy.wait()
    out[...] = jnp.where(me > 0, land[...], jnp.zeros_like(land))


def exchange(slot, device_of, src_of, land, send, recv):
    def copy(off, at):
        to = lax.rem(slot + off, 4)
        return pltpu.make_async_remote_copy(
            src_ref=src_of(to),
            dst_ref=land.at[at(to)],
            send_sem=send.at[off - 1],
            recv_sem=recv.at[at(to)],
            device_id={"seq": device_of(to)},
            device_id_type=MESH,
        )

    out = [copy(off, lambda to: slot) for off in range(1, 4)]
    for c in out:
        c.start()
    return out, [copy(off, lambda to: to) for off in range(1, 4)]


def layer_kernel(
    halo, q, k, v, gate, qt, kt, vt, blt, dlt, gain, w,
    out,
    halo_v, q_v, k_v, v_v, gate_v, qt_v, kt_v, vt_v, bl_v, dl_v, gain_v, w_v, in_sem,
    ext, cols_s, oloc, qeff, pair, gs,
    buf1, tot, buf2, rowt, buf3, outb, sin,
    s1, r1, s2, r2, s3, r3, s4, r4,
    nrm, part, land, psum, relay, final_s, from_lo, from_hi,
    sa, ra, sr, rr, sd, rd, sf, rf,
):
    pairs_in = (
        (dlt, dl_v), (blt, bl_v), (halo, halo_v), (kt, kt_v), (k, k_v), (vt, vt_v), (v, v_v),
        (qt, qt_v), (q, q_v), (gate, gate_v), (gain, gain_v), (w, w_v),
    )
    loads = {}
    for i, (src, dst) in enumerate(pairs_in):
        loads[i] = pltpu.make_async_copy(src, dst, in_sem.at[i])
        loads[i].start()
    me, l, g, x = place()
    hd = lax.axis_index("head")
    y, core = hd // 2, lax.rem(hd, 2)
    at_l = lambda i: me - l + i
    at_g = lambda i: me + (i - g) * NL
    at_x = lambda i: me + (i - x) * (NL * NG)
    sibling = {"head": hd + 1 - 2 * core}
    up = {"head": 2 * lax.rem(y + 1, NY) + core}
    down = {"head": 2 * lax.rem(y + NY - 1, NY) + core}
    peers = [sibling, up, down]
    for off in range(1, 4):
        peers.append({"seq": at_g(lax.rem(g + off, NG))})
        peers.append({"seq": at_l(lax.rem(l + off, NL))})
        peers.append({"seq": at_x(lax.rem(x + off, NX))})
    signal_all(peers)

    T = k.shape[0]
    nc = T // C
    qc, kc, vc = q.shape[1], k.shape[1], v.shape[1]
    nk, nv = kc // C, vc // C
    rep = nv // nk
    sl = lambda c: slice(c * C, (c + 1) * C)

    loads[0].wait()
    loads[1].wait()
    row = lax.broadcasted_iota(jnp.int32, (T, T), 0)
    col = lax.broadcasted_iota(jnp.int32, (T, T), 1)
    upto = (row <= col).astype(BF)
    dec = -softplus(dl_v[...])
    d1 = dec.astype(BF)
    r = dec - d1.astype(F32)
    d2 = r.astype(BF)
    d3 = (r - d2.astype(F32)).astype(BF)
    lfr = bdot(d1, upto) + bdot(d2, upto) + bdot(d3, upto)
    last = lfr[:, T - 1 : T]
    cols_s[0:4, :] = 1.0 / (1.0 + jnp.exp(-bl_v[...]))
    cols_s[4:8, :] = lfr
    cols_s[8:12, :] = jnp.exp(lfr)
    cols_s[12:16, :] = jnp.exp(last - lfr)
    cols = jnp.transpose(cols_s[...])
    beta = lambda h, c: cols[sl(c), h : h + 1]
    lf = lambda h, c: cols[sl(c), 4 + h : 5 + h]
    ex = lambda h, c: cols[sl(c), 8 + h : 9 + h]
    tail = lambda h, c: cols[sl(c), 12 + h : 13 + h]
    f1 = jnp.exp(last) - 1.0

    ri = lax.broadcasted_iota(jnp.int32, (C, C), 0)
    ci = lax.broadcasted_iota(jnp.int32, (C, C), 1)
    eye = (ri == ci).astype(F32)
    strict = ri > ci
    within = ri >= ci

    def put(lo, raw):
        wide = raw.shape[1]
        ext[5:8, lo : lo + wide] = halo_v[HALO - 3 : HALO, lo : lo + wide].astype(F32)
        ext[8 : 8 + T, lo : lo + wide] = raw[...].astype(F32)

    def conv(lo, taps, at):
        s = taps[0:1, at : at + C] * ext[5 : 5 + T, lo : lo + C]
        for j in range(1, 4):
            s = s + taps[j : j + 1, at : at + C] * ext[5 + j : 5 + j + T, lo : lo + C]
        return silu(s)

    loads[2].wait()
    loads[3].wait()
    loads[4].wait()
    put(qc, k_v)
    ks, KK, kT = [], [], []
    for j in range(nk):
        kj = conv(qc + j * C, kt_v, j * C)
        kj = kj * lax.rsqrt(jnp.sum(kj * kj, -1, keepdims=True) + EPS)
        kb = kj.astype(BF)
        ks.append(kb)
        kT.append(jnp.transpose(kj).astype(BF))
        KK.append({(c, e): bdot_nt(kb[sl(c)], kb[sl(e)]) for c in range(nc) for e in range(c + 1)})
    G = {}
    A = {}
    for h in range(nv):
        for c in range(nc):
            for e in range(c + 1):
                gap = jnp.exp(jnp.minimum(lf(h, c) - lfr[h : h + 1, sl(e)], 0.0))
                G[h, c, e] = gap
                a = (beta(h, c) * gap) * KK[h // rep][c, e]
                A[h, c, e] = jnp.where(strict, a, 0.0) if c == e else a

    keys = [(h, c) for h in range(nv) for c in range(nc)]

    def corner(s):
        return ((ri // (2 * s)) == (ci // (2 * s))) & ((ri // s) % 2 == 1) & ((ci // s) % 2 == 0)

    m = corner(1)
    inv = {(h, c): eye - jnp.where(m, A[h, c, c], 0.0) for h, c in keys}
    s = 2
    while s < C:
        m = corner(s)
        half = {(h, c): bdot(jnp.where(m, A[h, c, c], 0.0), inv[h, c]) for h, c in keys}
        inv = {key: inv[key] - bdot(inv[key], half[key]) for key in keys}
        s *= 2

    loads[5].wait()
    loads[6].wait()
    put(qc + kc, v_v)
    X = {}
    vs = [conv(qc + kc + h * C, vt_v, h * C) for h in range(nv)]
    for c in range(nc):
        rhs = {}
        for h in range(nv):
            kf = ks[h // rep][sl(c)].astype(F32)
            R = jnp.concatenate([beta(h, c) * vs[h][sl(c)], (beta(h, c) * ex(h, c)) * kf], 1)
            for e in range(c):
                R = R - bdot(A[h, c, e], X[h, e])
            rhs[h] = R
        for h in range(nv):
            X[h, c] = bdot(inv[h, c], rhs[h])
    for h in range(nv):
        hw = bdot(kT[h // rep][:, sl(0)], tail(h, 0) * X[h, 0])
        for c in range(1, nc):
            hw = hw + bdot(kT[h // rep][:, sl(c)], tail(h, c) * X[h, c])
        pair[h, :, :C] = (f1[h : h + 1, :] * eye - hw[:, C:]).astype(BF)
        pair[h, :, C:] = hw[:, :C].astype(BF)

    wait_all(len(peers))
    c1, w1 = exchange(l, at_l, lambda i: pair.at[i], buf1, s1, r1)
    buf1[l] = pair[l]

    loads[7].wait()
    loads[8].wait()
    put(0, q_v)
    for j in range(nk):
        qj = conv(j * C, qt_v, j * C)
        qb = qj.astype(BF)
        for c in range(nc):
            QK = {e: bdot_nt(qb[sl(c)], ks[j][sl(e)]) for e in range(c + 1)}
            for h in range(j * rep, (j + 1) * rep):
                ow = None
                for e in range(c + 1):
                    sc = G[h, c, e] * QK[e]
                    if c == e:
                        sc = jnp.where(within, sc, 0.0)
                    p = bdot(sc, X[h, e])
                    ow = p if ow is None else ow + p
                oloc[h, sl(c), :] = ow[:, :C]
                qeff[h, sl(c), :] = (ex(h, c) * qj[sl(c)] - ow[:, C:]).astype(BF)

    for copy in w1:
        copy.wait_recv()
    e0, e1, e2, e3 = [buf1[i].astype(F32) for i in range(NL)]
    p2 = compose(e1, e0)
    tot[...] = compose(compose(e3, e2), p2).astype(BF)
    c2, w2 = exchange(g, at_g, lambda i: tot, buf2, s2, r2)
    buf2[g] = tot[...]
    p3 = compose(e2, p2)

    loads[9].wait()
    loads[10].wait()
    for h in range(nv):
        gs[:, sl(h)] = gain_v[...] * silu(gate_v[:, sl(h)].astype(F32))

    for copy in w2:
        copy.wait_recv()
    g0, g1, g2, g3 = [buf2[i].astype(F32) for i in range(NG)]
    q2 = compose(g1, g0)
    rowt[...] = compose(compose(g3, g2), q2).astype(BF)
    c3, w3 = exchange(x, at_x, lambda i: rowt, buf3, s3, r3)
    buf3[x] = rowt[...]
    q3 = compose(g2, q2)
    zero = jnp.zeros((C, 2 * C), F32)
    gp = jnp.where(g == 0, zero, jnp.where(g == 1, g0, jnp.where(g == 2, q2, q3)))
    full = [gp] + [compose(p, gp) for p in (e0, p2, p3)]

    for copy in w3:
        copy.wait_recv()
    state1 = buf3[0, :, C:].astype(F32)
    state2 = applied(buf3[1].astype(F32), state1)
    state3 = applied(buf3[2].astype(F32), state2)
    row_in = jnp.where(
        x == 0, zero[:, :C], jnp.where(x == 1, state1, jnp.where(x == 2, state2, state3))
    )
    for i in range(NL):
        outb[i] = applied(full[i], row_in).astype(BF)
    c4, w4 = exchange(l, at_l, lambda i: outb.at[i], sin, s4, r4)
    sin[l] = outb[l]
    loads[11].wait()
    for copy in w4:
        copy.wait_recv()

    for h in range(nv):
        o = oloc[h] + bdot(qeff[h], sin[h])
        o = o * lax.rsqrt(jnp.mean(o * o, -1, keepdims=True) + EPS)
        nrm[:, sl(h)] = (o * gs[:, sl(h)]).astype(BF)

    wide = w.shape[1] // CH
    rows = T // 8

    def remote(src, dst, send, recv, device):
        return pltpu.make_async_remote_copy(
            src_ref=src, dst_ref=dst, send_sem=send, recv_sem=recv,
            device_id=device, device_id_type=MESH,
        )

    y_up, y_down, y_far = lax.rem(y + 1, NY), lax.rem(y + NY - 1, NY), lax.rem(y + 2, NY)
    within_chip = [
        remote(part.at[n, 1 - core], land.at[n], sa.at[n], ra.at[n], sibling) for n in range(CH)
    ]
    for n in range(CH):
        p = bdot(nrm[...], w_v[:, n * wide : (n + 1) * wide]).astype(BF)
        for b in range(8):
            part[n, b % 2, b // 2] = p[b * rows : (b + 1) * rows]
        within_chip[n].start()
    far, direct, last_hop = [], [], []
    for n in range(CH):
        a_dev, b_dev = (up, down) if n % 2 == 0 else (down, up)
        a_y, b_y = (y_up, y_down) if n % 2 == 0 else (y_down, y_up)
        a_land, b_land = (from_lo, from_hi) if n % 2 == 0 else (from_hi, from_lo)
        far.append(remote(psum.at[n, y_far], relay.at[n], sr.at[n], rr.at[n], a_dev))
        direct.append(remote(psum.at[n, b_y], b_land.at[n], sd.at[n], rd.at[n], b_dev))
        last_hop.append(remote(final_s.at[n], a_land.at[n], sf.at[n], rf.at[n], a_dev))
    for n in range(CH):
        within_chip[n].wait_recv()
        psum[n] = (part[n, core].astype(F32) + land[n].astype(F32)).astype(BF)
        far[n].start()
        direct[n].start()
    for n in range(CH):
        a_y = y_up if n % 2 == 0 else y_down
        far[n].wait_recv()
        final_s[n] = (psum[n, a_y].astype(F32) + relay[n].astype(F32)).astype(BF)
        last_hop[n].start()
    for n in range(CH):
        direct[n].wait_recv()
        last_hop[n].wait_recv()
        t = psum[n, y].astype(F32) + from_lo[n].astype(F32) + from_hi[n].astype(F32)
        out[:, n * wide : (n + 1) * wide] = t.astype(BF)
    for copy in c1 + c2 + c3 + c4 + within_chip + far + direct + last_hop:
        copy.wait_send()


def shards(q, k, v, gate, qt, kt, vt, bl, dl, gain, w):
    D = pltpu.SemaphoreType.DMA
    V = pltpu.VMEM
    any_space = pl.BlockSpec(memory_space=pl.ANY)
    vmem = pl.BlockSpec(memory_space=pltpu.VMEM)
    T = q.shape[0]
    wide_in = q.shape[1] + k.shape[1] + v.shape[1]
    halo = pl.pallas_call(
        halo_kernel,
        out_shape=jax.ShapeDtypeStruct((HALO, wide_in), BF),
        in_specs=[any_space] * 3,
        out_specs=vmem,
        scratch_shapes=[V((HALO, wide_in), BF), D((3,)), D((3,))],
        compiler_params=pltpu.CompilerParams(
            collective_id=1, has_side_effects=True, vmem_limit_bytes=60 << 20
        ),
        name="halo",
    )(q, k, v)
    args = (halo, q, k, v, gate, qt, kt, vt, bl.T, dl.T, gain.reshape(1, C), w)
    nv = v.shape[1] // C
    r, wide = T // 8, w.shape[1] // CH
    chunk = V((CH, r, wide), BF)
    four = V((CH, NY, r, wide), BF)
    scratch = [V(a.shape, a.dtype) for a in args]
    scratch += [D((len(args),))]
    scratch += [
        V((T + 8, wide_in), F32), V((16, T), F32), V((nv, T, C), F32), V((nv, T, C), BF),
        V((nv, C, 2 * C), BF), V((T, nv * C), F32),
    ]
    slots = V((4, C, 2 * C), BF)
    scratch += [slots, V((C, 2 * C), BF), slots, V((C, 2 * C), BF), slots]
    scratch += [V((4, C, C), BF), V((4, C, C), BF)]
    scratch += [D((3,)), D((4,))] * 4
    scratch += [V((T, nv * C), BF), V((CH, 2, NY, r, wide), BF), four, four]
    scratch += [chunk] * 4 + [D((CH,))] * 8
    return pl.pallas_call(
        layer_kernel,
        out_shape=jax.ShapeDtypeStruct((r, w.shape[1]), BF),
        in_specs=[any_space] * len(args),
        out_specs=vmem,
        scratch_shapes=scratch,
        compiler_params=pltpu.CompilerParams(
            collective_id=2, has_side_effects=True, vmem_limit_bytes=60 << 20
        ),
        name="layer",
    )(*args)


def solution(mesh):
    tokens_heads = P("seq", "head")
    placed = (tokens_heads,) * 4 + (P(None, "head"),) * 3 + (tokens_heads,) * 2
    return jax.shard_map(
        shards,
        mesh=mesh,
        in_specs=placed + (P(), P("head", None)),
        out_specs=P(("seq", "head"), None),
        check_vma=False,
    )
```

time: 722 us -> 68.5 us (0.09)
  waiting for transfers between devices: 502 us -> 0 us
  other arithmetic: 127 us -> 0 us
  Pallas kernels: 0 us -> 66.7 us
  matrix products: 46.4 us -> 0 us
  local copies, waits for them, and re-layouts: 17.7 us -> 1.62 us
  between operations: 13.5 us -> 0.02 us
  starting transfers between devices: 11.7 us -> 0 us
    all_gather x2 -> x0, waiting for transfers between devices: 379 us -> none  [carried_in(): gathered = jax.tree.map(lambda a: lax.all_gather(a, axis), part)]
    reduce_scatter x1 -> x0, waiting for transfers between devices: 123 us -> none  [shards(): lax.psum_scatter(jnp.dot(normed, out_weight, preferred_element_type=jnp.f...]
    another operation x3 -> x0, other arithmetic: 120 us -> none  [the longest x2 119 us: block_parts(): lax.linalg.triangular_solve(system, rhs_both, left_side=True, lower=True,...]
    pallas_call x0 -> x2, Pallas kernels: none -> 66.7 us  [the longest x1 50.9 us: shards(): pl.pallas_call(layer_kernel, out_shape=jax.ShapeDtypeStruct((r, w.shape[1...]
    dot_general x26 -> x0, matrix products: 44.8 us -> none  [the longest x18 25.2 us: stack_mul(): return jnp.einsum('bkl,blv->bkv', left, right, precision=PRECISE)]
    ppermute x3 -> x0, starting transfers between devices: 11.6 us -> none  [passed_along(): return lax.ppermute(value, axis, pairs)]
  transfers between devices with their start and end apart: 6 -> 0, of which waited for: 3 -> 0; matrix products, arithmetic and copies ran while one was open for 19% -> 0% of each run, Pallas kernels for 0% -> 0%
where the time goes in v3:
time: 68.5 us; the launch traced here: 68.3 us
  Pallas kernels  66.7 us (97%)
  local copies, waits for them, and re-layouts  1.62 us (2%)
    pallas_call x1, Pallas kernels, shards(): pl.pallas_call(layer_kernel, out_shape=jax.ShapeDtypeStruct((r, w.shape[1...  50.9 us
    pallas_call x1, Pallas kernels, shards(): pl.pallas_call(halo_kernel, out_shape=jax.ShapeDtypeStruct((HALO, wide_in...  15.8 us
    unnamed x1, local copies, waits for them, and re-layouts  1.62 us

profile of v3, /device:TPU:1, one launch (start us, length us, event | category | flops | bytes accessed | tf_op | source)
XLA Modules:
  0.0 68.3 jit_solution(17413677728883393710)
XLA Ops:
  0.0 15.8 %halo.1 = bf16[16,1024]{1,0:T(8,128)(2,1)} custom-call(bf16[384,256]{1,0:T(8,128)(2,1)} %q.3, bf16[384,256]{1,0:T(8,128)(2,1)} %k.3, bf16[384,512]{1,0:T(8,128)(2,1)} %v.3), custom_call_target="tpu_custom_call" | custom-call | tf_op jit(solution)/shard_map/halo/pallas_call | solution.py:374
  15.8 50.9 %layer.1 = bf16[48,2048]{1,0:T(8,128)(2,1)} custom-call(bf16[16,1024]{1,0:T(8,128)(2,1)} %halo.1, bf16[384,256]{1,0:T(8,128)(2,1)} %q.3, bf16[384,256]{1,0:T(8,128)(2,1)} %k.3, bf16[384,512]{1,0:T(8,128)(2,1)} %v.3, bf16[384,512]{1,0:T(8,128)(2,1)} %gate.1, f32[4,256]{1,0:T(4,128)} %qt.1, f32[4,256]{1,0:T(4,128)} %kt.1, f32[4,512]{1,0:T(4,128)} %vt.1, ...), custom_call_target="tpu_custom_call" | custom-call | tf_op jit(solution)/shard_map/layer/pallas_call | solution.py:402
  66.7 1.6 %copy.13 = bf16[48,2048]{1,0:T(8,128)(2,1)} copy(bf16[48,2048]{1,0:T(8,128)(2,1)} %layer.1) | data formatting | bytes 393216

commit v4 on v3

--- a/solution.py
+++ b/solution.py
@@ -64,34 +64,6 @@
     pl.semaphore_wait(pltpu.get_barrier_semaphore(), count)
 
 
-def halo_kernel(q, k, v, out, land, send, recv):
-    me = lax.axis_index("seq")
-    n = lax.axis_size("seq")
-    after = {"seq": lax.rem(me + 1, n)}
-    before = {"seq": lax.rem(me + n - 1, n)}
-    signal_all([after, before])
-    wait_all(2)
-    copies = []
-    lo = 0
-    for i, ref in enumerate((q, k, v)):
-        t, w = ref.shape
-        copies.append(
-            pltpu.make_async_remote_copy(
-                src_ref=ref.at[pl.ds(t - HALO, HALO)],
-                dst_ref=land.at[:, pl.ds(lo, w)],
-                send_sem=send.at[i],
-                recv_sem=recv.at[i],
-                device_id=after,
-                device_id_type=MESH,
-            )
-        )
-        copies[-1].start()
-        lo += w
-    for copy in copies:
-        copy.wait()
-    out[...] = jnp.where(me > 0, land[...], jnp.zeros_like(land))
-
-
 def exchange(slot, device_of, src_of, land, send, recv):
     def copy(off, at):
         to = lax.rem(slot + off, 4)
@@ -111,17 +83,18 @@
 
 
 def layer_kernel(
-    halo, q, k, v, gate, qt, kt, vt, blt, dlt, gain, w,
+    q, k, v, gate, qt, kt, vt, blt, dlt, gain, w,
     out,
-    halo_v, q_v, k_v, v_v, gate_v, qt_v, kt_v, vt_v, bl_v, dl_v, gain_v, w_v, in_sem,
+    q_v, k_v, v_v, gate_v, qt_v, kt_v, vt_v, bl_v, dl_v, gain_v, w_v, in_sem,
+    halo_v, w_sib, sh, rh, sw, rw,
     ext, cols_s, oloc, qeff, pair, gs,
     buf1, tot, buf2, rowt, buf3, outb, sin,
     s1, r1, s2, r2, s3, r3, s4, r4,
-    nrm, part, land, psum, relay, final_s, from_lo, from_hi,
+    nrm, n_sib, acc, psum, relay, final_s, from_lo, from_hi,
     sa, ra, sr, rr, sd, rd, sf, rf,
 ):
     pairs_in = (
-        (dlt, dl_v), (blt, bl_v), (halo, halo_v), (kt, kt_v), (k, k_v), (vt, vt_v), (v, v_v),
+        (dlt, dl_v), (blt, bl_v), (kt, kt_v), (k, k_v), (vt, vt_v), (v, v_v),
         (qt, qt_v), (q, q_v), (gate, gate_v), (gain, gain_v), (w, w_v),
     )
     loads = {}
@@ -142,7 +115,17 @@
         peers.append({"seq": at_g(lax.rem(g + off, NG))})
         peers.append({"seq": at_l(lax.rem(l + off, NL))})
         peers.append({"seq": at_x(lax.rem(x + off, NX))})
+    n_seq = lax.axis_size("seq")
+    after = {"seq": lax.rem(me + 1, n_seq)}
+    before = {"seq": lax.rem(me + n_seq - 1, n_seq)}
+    peers += [after, before]
     signal_all(peers)
+
+    def remote(src, dst, send, recv, device):
+        return pltpu.make_async_remote_copy(
+            src_ref=src, dst_ref=dst, send_sem=send, recv_sem=recv,
+            device_id=device, device_id_type=MESH,
+        )
 
     T = k.shape[0]
     nc = T // C
@@ -180,87 +163,111 @@
     strict = ri > ci
     within = ri >= ci
 
+    wait_all(len(peers))
+    sent_halo = []
+    lo = 0
+    for i, ref in enumerate((q, k, v)):
+        span = pl.ds(lo, ref.shape[1])
+        sent_halo.append(
+            remote(ref.at[pl.ds(T - HALO, HALO)], halo_v.at[:, span], sh.at[i], rh.at[i], after)
+        )
+        lo += ref.shape[1]
+    for copy in sent_halo:
+        copy.start()
+    sent_w = remote(w, w_sib, sw.at[0], rw.at[0], sibling)
+    sent_w.start()
+
     def put(lo, raw):
         wide = raw.shape[1]
-        ext[5:8, lo : lo + wide] = halo_v[HALO - 3 : HALO, lo : lo + wide].astype(F32)
         ext[8 : 8 + T, lo : lo + wide] = raw[...].astype(F32)
 
-    def conv(lo, taps, at):
-        s = taps[0:1, at : at + C] * ext[5 : 5 + T, lo : lo + C]
+    def conv(lo, taps, at, c, n=1):
+        s = taps[0:1, at : at + C] * ext[5 + c * C : 5 + (c + n) * C, lo : lo + C]
         for j in range(1, 4):
-            s = s + taps[j : j + 1, at : at + C] * ext[5 + j : 5 + j + T, lo : lo + C]
+            s = s + taps[j : j + 1, at : at + C] * ext[5 + j + c * C : 5 + j + (c + n) * C, lo : lo + C]
         return silu(s)
 
-    loads[2].wait()
-    loads[3].wait()
-    loads[4].wait()
+    for i in range(2, 6):
+        loads[i].wait()
     put(qc, k_v)
-    ks, KK, kT = [], [], []
-    for j in range(nk):
-        kj = conv(qc + j * C, kt_v, j * C)
-        kj = kj * lax.rsqrt(jnp.sum(kj * kj, -1, keepdims=True) + EPS)
-        kb = kj.astype(BF)
-        ks.append(kb)
-        kT.append(jnp.transpose(kj).astype(BF))
-        KK.append({(c, e): bdot_nt(kb[sl(c)], kb[sl(e)]) for c in range(nc) for e in range(c + 1)})
-    G = {}
-    A = {}
-    for h in range(nv):
-        for c in range(nc):
-            for e in range(c + 1):
-                gap = jnp.exp(jnp.minimum(lf(h, c) - lfr[h : h + 1, sl(e)], 0.0))
-                G[h, c, e] = gap
-                a = (beta(h, c) * gap) * KK[h // rep][c, e]
-                A[h, c, e] = jnp.where(strict, a, 0.0) if c == e else a
-
-    keys = [(h, c) for h in range(nv) for c in range(nc)]
+    put(qc + kc, v_v)
+    ks, kT, vs, KK, G, A = {}, {}, {}, {}, {}, {}
+
+    def block(c):
+        for j in range(nk):
+            kj = conv(qc + j * C, kt_v, j * C, c)
+            kj = kj * lax.rsqrt(jnp.sum(kj * kj, -1, keepdims=True) + EPS)
+            ks[j, c] = kj.astype(BF)
+            kT[j, c] = jnp.transpose(kj).astype(BF)
+        for h in range(nv):
+            vs[h, c] = conv(qc + kc + h * C, vt_v, h * C, c)
+
+    def system(c, e):
+        for j in range(nk):
+            KK[j] = bdot_nt(ks[j, c], ks[j, e])
+        for h in range(nv):
+            G[h, c, e] = jnp.exp(jnp.minimum(lf(h, c) - lfr[h : h + 1, sl(e)], 0.0))
+            a = (beta(h, c) * G[h, c, e]) * KK[h // rep]
+            A[h, c, e] = jnp.where(strict, a, 0.0) if c == e else a
 
     def corner(s):
         return ((ri // (2 * s)) == (ci // (2 * s))) & ((ri // s) % 2 == 1) & ((ci // s) % 2 == 0)
 
-    m = corner(1)
-    inv = {(h, c): eye - jnp.where(m, A[h, c, c], 0.0) for h, c in keys}
-    s = 2
-    while s < C:
-        m = corner(s)
-        half = {(h, c): bdot(jnp.where(m, A[h, c, c], 0.0), inv[h, c]) for h, c in keys}
-        inv = {key: inv[key] - bdot(inv[key], half[key]) for key in keys}
-        s *= 2
-
-    loads[5].wait()
-    loads[6].wait()
-    put(qc + kc, v_v)
+    def inverses(keys):
+        m = corner(1)
+        out = {(h, c): eye - jnp.where(m, A[h, c, c], 0.0) for h, c in keys}
+        s = 2
+        while s < C:
+            m = corner(s)
+            part = {(h, c): bdot(jnp.where(m, A[h, c, c], 0.0), out[h, c]) for h, c in keys}
+            out = {key: out[key] - bdot(out[key], part[key]) for key in keys}
+            s *= 2
+        return out
+
+    for c in range(1, nc):
+        block(c)
+    for c in range(1, nc):
+        for e in range(1, c + 1):
+            system(c, e)
+    inv = inverses([(h, c) for h in range(nv) for c in range(1, nc)])
+    for copy in sent_halo:
+        copy.wait_recv()
+    start = halo_v[HALO - 3 : HALO, :].astype(F32)
+    ext[5:8, :] = jnp.where(me > 0, start, jnp.zeros_like(start))
+    block(0)
+    for c in range(nc):
+        system(c, 0)
+    inv.update(inverses([(h, 0) for h in range(nv)]))
+
     X = {}
-    vs = [conv(qc + kc + h * C, vt_v, h * C) for h in range(nv)]
     for c in range(nc):
         rhs = {}
         for h in range(nv):
-            kf = ks[h // rep][sl(c)].astype(F32)
-            R = jnp.concatenate([beta(h, c) * vs[h][sl(c)], (beta(h, c) * ex(h, c)) * kf], 1)
+            kf = ks[h // rep, c].astype(F32)
+            R = jnp.concatenate([beta(h, c) * vs[h, c], (beta(h, c) * ex(h, c)) * kf], 1)
             for e in range(c):
                 R = R - bdot(A[h, c, e], X[h, e])
             rhs[h] = R
         for h in range(nv):
             X[h, c] = bdot(inv[h, c], rhs[h])
     for h in range(nv):
-        hw = bdot(kT[h // rep][:, sl(0)], tail(h, 0) * X[h, 0])
+        hw = bdot(kT[h // rep, 0], tail(h, 0) * X[h, 0])
         for c in range(1, nc):
-            hw = hw + bdot(kT[h // rep][:, sl(c)], tail(h, c) * X[h, c])
+            hw = hw + bdot(kT[h // rep, c], tail(h, c) * X[h, c])
         pair[h, :, :C] = (f1[h : h + 1, :] * eye - hw[:, C:]).astype(BF)
         pair[h, :, C:] = hw[:, :C].astype(BF)
 
-    wait_all(len(peers))
     c1, w1 = exchange(l, at_l, lambda i: pair.at[i], buf1, s1, r1)
     buf1[l] = pair[l]
 
+    loads[6].wait()
     loads[7].wait()
-    loads[8].wait()
     put(0, q_v)
     for j in range(nk):
-        qj = conv(j * C, qt_v, j * C)
+        qj = conv(j * C, qt_v, j * C, 0, nc)
         qb = qj.astype(BF)
         for c in range(nc):
-            QK = {e: bdot_nt(qb[sl(c)], ks[j][sl(e)]) for e in range(c + 1)}
+            QK = {e: bdot_nt(qb[sl(c)], ks[j, e]) for e in range(c + 1)}
             for h in range(j * rep, (j + 1) * rep):
                 ow = None
                 for e in range(c + 1):
@@ -281,8 +288,8 @@
     buf2[g] = tot[...]
     p3 = compose(e2, p2)
 
+    loads[8].wait()
     loads[9].wait()
-    loads[10].wait()
     for h in range(nv):
         gs[:, sl(h)] = gain_v[...] * silu(gate_v[:, sl(h)].astype(F32))
 
@@ -310,33 +317,36 @@
         outb[i] = applied(full[i], row_in).astype(BF)
     c4, w4 = exchange(l, at_l, lambda i: outb.at[i], sin, s4, r4)
     sin[l] = outb[l]
-    loads[11].wait()
+    loads[10].wait()
     for copy in w4:
         copy.wait_recv()
 
-    for h in range(nv):
-        o = oloc[h] + bdot(qeff[h], sin[h])
-        o = o * lax.rsqrt(jnp.mean(o * o, -1, keepdims=True) + EPS)
-        nrm[:, sl(h)] = (o * gs[:, sl(h)]).astype(BF)
-
+    rows = T // 8
     wide = w.shape[1] // CH
-    rows = T // 8
-
-    def remote(src, dst, send, recv, device):
-        return pltpu.make_async_remote_copy(
-            src_ref=src, dst_ref=dst, send_sem=send, recv_sem=recv,
-            device_id=device, device_id_type=MESH,
-        )
+    half = nv * C // 2
+    swap = [remote(nrm.at[i, 1 - core], n_sib.at[i], sa.at[i], ra.at[i], sibling) for i in range(2)]
+    for i in range(2):
+        for h in range(i * nv // 2, (i + 1) * nv // 2):
+            o = oloc[h] + bdot(qeff[h], sin[h])
+            o = o * lax.rsqrt(jnp.mean(o * o, -1, keepdims=True) + EPS)
+            o = (o * gs[:, sl(h)]).astype(BF)
+            at = h * C - i * half
+            for b in range(8):
+                nrm[i, b % 2, b // 2, :, at : at + C] = o[b * rows : (b + 1) * rows]
+        swap[i].start()
+
+    def lhs(ref):
+        return ref.reshape(NY * rows, half)
+
+    mine = jnp.concatenate([lhs(nrm[0, core]), lhs(nrm[1, core])], 1)
+    for n in range(CH):
+        acc[:, n * wide : (n + 1) * wide] = bdot(mine, w_v[:, n * wide : (n + 1) * wide])
+    sent_w.wait_recv()
+    for copy in swap:
+        copy.wait_recv()
+    other = jnp.concatenate([lhs(n_sib[0]), lhs(n_sib[1])], 1)
 
     y_up, y_down, y_far = lax.rem(y + 1, NY), lax.rem(y + NY - 1, NY), lax.rem(y + 2, NY)
-    within_chip = [
-        remote(part.at[n, 1 - core], land.at[n], sa.at[n], ra.at[n], sibling) for n in range(CH)
-    ]
-    for n in range(CH):
-        p = bdot(nrm[...], w_v[:, n * wide : (n + 1) * wide]).astype(BF)
-        for b in range(8):
-            part[n, b % 2, b // 2] = p[b * rows : (b + 1) * rows]
-        within_chip[n].start()
     far, direct, last_hop = [], [], []
     for n in range(CH):
         a_dev, b_dev = (up, down) if n % 2 == 0 else (down, up)
@@ -346,9 +356,11 @@
         direct.append(remote(psum.at[n, b_y], b_land.at[n], sd.at[n], rd.at[n], b_dev))
         last_hop.append(remote(final_s.at[n], a_land.at[n], sf.at[n], rf.at[n], a_dev))
     for n in range(CH):
-        within_chip[n].wait_recv()
-        psum[n] = (part[n, core].astype(F32) + land[n].astype(F32)).astype(BF)
+        at = slice(n * wide, (n + 1) * wide)
+        total = acc[:, at] + bdot(other, w_sib[:, at])
+        psum[n] = total.astype(BF).reshape(NY, rows, wide)
         far[n].start()
+    for n in range(CH):
         direct[n].start()
     for n in range(CH):
         a_y = y_up if n % 2 == 0 else y_down
@@ -360,35 +372,25 @@
         last_hop[n].wait_recv()
         t = psum[n, y].astype(F32) + from_lo[n].astype(F32) + from_hi[n].astype(F32)
         out[:, n * wide : (n + 1) * wide] = t.astype(BF)
-    for copy in c1 + c2 + c3 + c4 + within_chip + far + direct + last_hop:
+    for copy in sent_halo + [sent_w] + c1 + c2 + c3 + c4 + swap + far + direct + last_hop:
         copy.wait_send()
 
 
 def shards(q, k, v, gate, qt, kt, vt, bl, dl, gain, w):
     D = pltpu.SemaphoreType.DMA
     V = pltpu.VMEM
-    any_space = pl.BlockSpec(memory_space=pl.ANY)
+    hbm = pl.BlockSpec(memory_space=pltpu.HBM)
     vmem = pl.BlockSpec(memory_space=pltpu.VMEM)
     T = q.shape[0]
     wide_in = q.shape[1] + k.shape[1] + v.shape[1]
-    halo = pl.pallas_call(
-        halo_kernel,
-        out_shape=jax.ShapeDtypeStruct((HALO, wide_in), BF),
-        in_specs=[any_space] * 3,
-        out_specs=vmem,
-        scratch_shapes=[V((HALO, wide_in), BF), D((3,)), D((3,))],
-        compiler_params=pltpu.CompilerParams(
-            collective_id=1, has_side_effects=True, vmem_limit_bytes=60 << 20
-        ),
-        name="halo",
-    )(q, k, v)
-    args = (halo, q, k, v, gate, qt, kt, vt, bl.T, dl.T, gain.reshape(1, C), w)
+    args = (q, k, v, gate, qt, kt, vt, bl.T, dl.T, gain.reshape(1, C), w)
     nv = v.shape[1] // C
     r, wide = T // 8, w.shape[1] // CH
     chunk = V((CH, r, wide), BF)
     four = V((CH, NY, r, wide), BF)
     scratch = [V(a.shape, a.dtype) for a in args]
-    scratch += [D((len(args),))]
+    scratch += [D((len(args),)), V((HALO, wide_in), BF), V(w.shape, BF)]
+    scratch += [D((3,)), D((3,)), D((1,)), D((1,))]
     scratch += [
         V((T + 8, wide_in), F32), V((16, T), F32), V((nv, T, C), F32), V((nv, T, C), BF),
         V((nv, C, 2 * C), BF), V((T, nv * C), F32),
@@ -397,19 +399,20 @@
     scratch += [slots, V((C, 2 * C), BF), slots, V((C, 2 * C), BF), slots]
     scratch += [V((4, C, C), BF), V((4, C, C), BF)]
     scratch += [D((3,)), D((4,))] * 4
-    scratch += [V((T, nv * C), BF), V((CH, 2, NY, r, wide), BF), four, four]
-    scratch += [chunk] * 4 + [D((CH,))] * 8
+    scratch += [V((2, 2, NY, r, nv * C // 2), BF), V((2, NY, r, nv * C // 2), BF)]
+    scratch += [V((NY * r, w.shape[1]), F32), four]
+    scratch += [chunk] * 4 + [D((2,))] * 2 + [D((CH,))] * 6
     return pl.pallas_call(
         layer_kernel,
         out_shape=jax.ShapeDtypeStruct((r, w.shape[1]), BF),
-        in_specs=[any_space] * len(args),
+        in_specs=[hbm] * len(args),
         out_specs=vmem,
         scratch_shapes=scratch,
         compiler_params=pltpu.CompilerParams(
-            collective_id=2, has_side_effects=True, vmem_limit_bytes=60 << 20
+            collective_id=2, has_side_effects=True, vmem_limit_bytes=48 << 20
         ),
         name="layer",
-    )(*args)
+    )(*[pltpu.with_memory_space_constraint(a, pltpu.HBM) for a in args])
 
 
 def solution(mesh):

time: 68.5 us -> 66.9 us (0.977)
  local copies, waits for them, and re-layouts: 1.62 us -> 0.68 us
  Pallas kernels: 66.7 us -> 66 us
    pallas_call x1 -> x0, Pallas kernels: 15.8 us -> none  [shards(): pl.pallas_call(halo_kernel, out_shape=jax.ShapeDtypeStruct((HALO, wide_in...]
    pallas_call x1, Pallas kernels: 50.9 us -> 66 us  [shards(): pl.pallas_call(layer_kernel, out_shape=jax.ShapeDtypeStruct((r, w.shape[1...]
    unnamed x1, local copies, waits for them, and re-layouts: 1.62 us -> 0.68 us
where the time goes in v4:
time: 66.9 us; the launch traced here: 66.7 us
  Pallas kernels  66 us (99%)
  local copies, waits for them, and re-layouts  0.68 us (1%)
    pallas_call x1, Pallas kernels, shards(): pl.pallas_call(layer_kernel, out_shape=jax.ShapeDtypeStruct((r, w.shape[1...  66 us

profile of v4, /device:TPU:1, one launch (start us, length us, event | category | flops | bytes accessed | tf_op | source)
XLA Modules:
  0.0 66.7 jit_solution(4942619102296696153)
XLA Ops:
  0.0 66.0 %layer.1 = bf16[48,2048]{1,0:T(8,128)(2,1)S(1)} custom-call(bf16[384,256]{1,0:T(8,128)(2,1)} %q.1, bf16[384,256]{1,0:T(8,128)(2,1)} %k.1, bf16[384,512]{1,0:T(8,128)(2,1)} %v.1, bf16[384,512]{1,0:T(8,128)(2,1)} %gate.1, f32[4,256]{1,0:T(4,128)} %qt.1, f32[4,256]{1,0:T(4,128)} %kt.1, f32[4,512]{1,0:T(4,128)} %vt.1, f32[4,384]{1,0:T(4,128)} %bitcast.3, ...), custom_call_target="tpu_custom_call" | custom-call | tf_op jit(solution)/shard_map/layer/pallas_call | solution.py:405
  66.0 0.7 %copy.13 = bf16[48,2048]{1,0:T(8,128)(2,1)} copy(bf16[48,2048]{1,0:T(8,128)(2,1)S(1)} %layer.1) | data formatting | bytes 393216

commit v5 on v4

--- a/solution.py
+++ b/solution.py
@@ -16,6 +16,7 @@
 NY = 4
 CH = 4
 HALO = 16
+EDGE = 8
 
 
 def bdot(a, b):
@@ -90,7 +91,7 @@
     ext, cols_s, oloc, qeff, pair, gs,
     buf1, tot, buf2, rowt, buf3, outb, sin,
     s1, r1, s2, r2, s3, r3, s4, r4,
-    nrm, n_sib, acc, psum, relay, final_s, from_lo, from_hi,
+    nrm, n_sib, psum, relay, final_s, from_lo, from_hi,
     sa, ra, sr, rr, sd, rd, sf, rf,
 ):
     pairs_in = (
@@ -213,23 +214,39 @@
     def corner(s):
         return ((ri // (2 * s)) == (ci // (2 * s))) & ((ri // s) % 2 == 1) & ((ci // s) % 2 == 0)
 
-    def inverses(keys):
+    def inverses(blocks, upto=C):
         m = corner(1)
-        out = {(h, c): eye - jnp.where(m, A[h, c, c], 0.0) for h, c in keys}
+        out = {key: eye - jnp.where(m, a, 0.0) for key, a in blocks.items()}
         s = 2
-        while s < C:
+        while s < upto:
             m = corner(s)
-            part = {(h, c): bdot(jnp.where(m, A[h, c, c], 0.0), out[h, c]) for h, c in keys}
-            out = {key: out[key] - bdot(out[key], part[key]) for key in keys}
+            part = {key: bdot(jnp.where(m, a, 0.0), out[key]) for key, a in blocks.items()}
+            out = {key: out[key] - bdot(out[key], part[key]) for key in blocks}
             s *= 2
         return out
 
-    for c in range(1, nc):
+    def rhs(h, c):
+        kf = ks[h // rep, c].astype(F32)
+        return jnp.concatenate([beta(h, c) * vs[h, c], (beta(h, c) * ex(h, c)) * kf], 1)
+
+    ext[0:8, :] = jnp.zeros((8, ext.shape[1]), F32)
+    inner = (ri >= EDGE) & (ci >= EDGE)
+    for c in range(nc):
         block(c)
-    for c in range(1, nc):
-        for e in range(1, c + 1):
+    for c in range(nc):
+        for e in range(min(c, 1), c + 1):
             system(c, e)
-    inv = inverses([(h, c) for h in range(nv) for c in range(1, nc)])
+    blocks = {(h, c): A[h, c, c] for h in range(nv) for c in range(1, nc)}
+    blocks.update({(h, 0): jnp.where(inner, A[h, 0, 0], 0.0) for h in range(nv)})
+    inv = inverses(blocks)
+    ahead, cross = {}, {}
+    for h in range(nv):
+        cross[h] = bdot(inv[h, 2], bdot(A[h, 2, 1], inv[h, 1]))
+    for h in range(nv):
+        b1, b2 = rhs(h, 1), rhs(h, 2)
+        ahead[h, 1] = bdot(inv[h, 1], b1)
+        ahead[h, 2] = bdot(inv[h, 2], b2) - bdot(cross[h], b1)
+
     for copy in sent_halo:
         copy.wait_recv()
     start = halo_v[HALO - 3 : HALO, :].astype(F32)
@@ -237,19 +254,18 @@
     block(0)
     for c in range(nc):
         system(c, 0)
-    inv.update(inverses([(h, 0) for h in range(nv)]))
-
+    edge = inverses({h: jnp.where(ri < EDGE, A[h, 0, 0], 0.0) for h in range(nv)}, EDGE)
     X = {}
-    for c in range(nc):
-        rhs = {}
-        for h in range(nv):
-            kf = ks[h // rep, c].astype(F32)
-            R = jnp.concatenate([beta(h, c) * vs[h, c], (beta(h, c) * ex(h, c)) * kf], 1)
-            for e in range(c):
-                R = R - bdot(A[h, c, e], X[h, e])
-            rhs[h] = R
-        for h in range(nv):
-            X[h, c] = bdot(inv[h, c], rhs[h])
+    part = {h: bdot(edge[h], rhs(h, 0)) for h in range(nv)}
+    for h in range(nv):
+        below = jnp.where((ri >= EDGE) & (ci < EDGE), A[h, 0, 0], 0.0)
+        part[h] = part[h] - bdot(below, part[h])
+    for h in range(nv):
+        X[h, 0] = bdot(inv[h, 0], part[h])
+    for h in range(nv):
+        b1, b2 = bdot(A[h, 1, 0], X[h, 0]), bdot(A[h, 2, 0], X[h, 0])
+        X[h, 1] = ahead[h, 1] - bdot(inv[h, 1], b1)
+        X[h, 2] = ahead[h, 2] - bdot(inv[h, 2], b2) + bdot(cross[h], b1)
     for h in range(nv):
         hw = bdot(kT[h // rep, 0], tail(h, 0) * X[h, 0])
         for c in range(1, nc):
@@ -307,14 +323,14 @@
 
     for copy in w3:
         copy.wait_recv()
-    state1 = buf3[0, :, C:].astype(F32)
-    state2 = applied(buf3[1].astype(F32), state1)
-    state3 = applied(buf3[2].astype(F32), state2)
-    row_in = jnp.where(
-        x == 0, zero[:, :C], jnp.where(x == 1, state1, jnp.where(x == 2, state2, state3))
-    )
+    after0 = buf3[0, :, C:].astype(F32)
+    after1 = applied(buf3[1].astype(F32), after0)
+    early = jnp.where(x == 2, after0, jnp.where(x == 3, after1, jnp.zeros_like(after0)))
+    late = buf3[lax.rem(x + NX - 1, NX)].astype(F32)
+    late = jnp.where(x > 0, late, jnp.zeros_like(late))
+    through = [compose(p, late) for p in full]
     for i in range(NL):
-        outb[i] = applied(full[i], row_in).astype(BF)
+        outb[i] = applied(through[i], early).astype(BF)
     c4, w4 = exchange(l, at_l, lambda i: outb.at[i], sin, s4, r4)
     sin[l] = outb[l]
     loads[10].wait()
@@ -323,54 +339,61 @@
 
     rows = T // 8
     wide = w.shape[1] // CH
-    half = nv * C // 2
-    swap = [remote(nrm.at[i, 1 - core], n_sib.at[i], sa.at[i], ra.at[i], sibling) for i in range(2)]
-    for i in range(2):
-        for h in range(i * nv // 2, (i + 1) * nv // 2):
-            o = oloc[h] + bdot(qeff[h], sin[h])
+    y_up, y_down, y_far = lax.rem(y + 1, NY), lax.rem(y + NY - 1, NY), lax.rem(y + 2, NY)
+
+    swap = [
+        remote(nrm.at[1 - core, pl.ds(0, 1)], n_sib.at[pl.ds(0, 1)], sa.at[0], ra.at[0], sibling),
+        remote(nrm.at[1 - core, pl.ds(1, 3)], n_sib.at[pl.ds(1, 3)], sa.at[1], ra.at[1], sibling),
+    ]
+
+    def normed(at, slot):
+        span = pl.ds(pl.multiple_of(at * 2 * rows, 2 * rows), 2 * rows)
+        for h in range(nv):
+            o = oloc[h, span, :] + bdot(qeff[h, span, :], sin[h])
             o = o * lax.rsqrt(jnp.mean(o * o, -1, keepdims=True) + EPS)
-            o = (o * gs[:, sl(h)]).astype(BF)
-            at = h * C - i * half
-            for b in range(8):
-                nrm[i, b % 2, b // 2, :, at : at + C] = o[b * rows : (b + 1) * rows]
-        swap[i].start()
-
-    def lhs(ref):
-        return ref.reshape(NY * rows, half)
-
-    mine = jnp.concatenate([lhs(nrm[0, core]), lhs(nrm[1, core])], 1)
-    for n in range(CH):
-        acc[:, n * wide : (n + 1) * wide] = bdot(mine, w_v[:, n * wide : (n + 1) * wide])
-    sent_w.wait_recv()
-    for copy in swap:
-        copy.wait_recv()
-    other = jnp.concatenate([lhs(n_sib[0]), lhs(n_sib[1])], 1)
-
-    y_up, y_down, y_far = lax.rem(y + 1, NY), lax.rem(y + NY - 1, NY), lax.rem(y + 2, NY)
+            o = (o * gs[span, sl(h)]).astype(BF)
+            for b in range(2):
+                nrm[b, slot, :, sl(h)] = o[b * rows : (b + 1) * rows]
+
+    def project(lo, hi, n):
+        at = slice(n * wide, (n + 1) * wide)
+        count = (hi - lo) * rows
+        mine = nrm[core, lo:hi].reshape(count, nv * C)
+        other = n_sib[lo:hi].reshape(count, nv * C)
+        total = bdot(mine, w_v[:, at]) + bdot(other, w_sib[:, at])
+        psum[n, lo:hi] = total.astype(BF).reshape(hi - lo, rows, wide)
+
     far, direct, last_hop = [], [], []
     for n in range(CH):
         a_dev, b_dev = (up, down) if n % 2 == 0 else (down, up)
-        a_y, b_y = (y_up, y_down) if n % 2 == 0 else (y_down, y_up)
+        b_slot = 2 if n % 2 == 0 else 1
         a_land, b_land = (from_lo, from_hi) if n % 2 == 0 else (from_hi, from_lo)
-        far.append(remote(psum.at[n, y_far], relay.at[n], sr.at[n], rr.at[n], a_dev))
-        direct.append(remote(psum.at[n, b_y], b_land.at[n], sd.at[n], rd.at[n], b_dev))
+        far.append(remote(psum.at[n, 0], relay.at[n], sr.at[n], rr.at[n], a_dev))
+        direct.append(remote(psum.at[n, b_slot], b_land.at[n], sd.at[n], rd.at[n], b_dev))
         last_hop.append(remote(final_s.at[n], a_land.at[n], sf.at[n], rf.at[n], a_dev))
+    normed(y_far, 0)
+    swap[0].start()
+    for slot, at in ((1, y_up), (2, y_down), (3, y)):
+        normed(at, slot)
+    swap[1].start()
+    sent_w.wait_recv()
+    swap[0].wait_recv()
     for n in range(CH):
-        at = slice(n * wide, (n + 1) * wide)
-        total = acc[:, at] + bdot(other, w_sib[:, at])
-        psum[n] = total.astype(BF).reshape(NY, rows, wide)
+        project(0, 1, n)
         far[n].start()
+    swap[1].wait_recv()
     for n in range(CH):
+        project(1, NY, n)
         direct[n].start()
     for n in range(CH):
-        a_y = y_up if n % 2 == 0 else y_down
+        a_slot = 1 if n % 2 == 0 else 2
         far[n].wait_recv()
-        final_s[n] = (psum[n, a_y].astype(F32) + relay[n].astype(F32)).astype(BF)
+        final_s[n] = (psum[n, a_slot].astype(F32) + relay[n].astype(F32)).astype(BF)
         last_hop[n].start()
     for n in range(CH):
         direct[n].wait_recv()
         last_hop[n].wait_recv()
-        t = psum[n, y].astype(F32) + from_lo[n].astype(F32) + from_hi[n].astype(F32)
+        t = psum[n, 3].astype(F32) + from_lo[n].astype(F32) + from_hi[n].astype(F32)
         out[:, n * wide : (n + 1) * wide] = t.astype(BF)
     for copy in sent_halo + [sent_w] + c1 + c2 + c3 + c4 + swap + far + direct + last_hop:
         copy.wait_send()
@@ -399,8 +422,7 @@
     scratch += [slots, V((C, 2 * C), BF), slots, V((C, 2 * C), BF), slots]
     scratch += [V((4, C, C), BF), V((4, C, C), BF)]
     scratch += [D((3,)), D((4,))] * 4
-    scratch += [V((2, 2, NY, r, nv * C // 2), BF), V((2, NY, r, nv * C // 2), BF)]
-    scratch += [V((NY * r, w.shape[1]), F32), four]
+    scratch += [V((2, NY, r, nv * C), BF), V((NY, r, nv * C), BF), four]
     scratch += [chunk] * 4 + [D((2,))] * 2 + [D((CH,))] * 6
     return pl.pallas_call(
         layer_kernel,

time: 66.9 us -> 65.5 us (0.979)
  Pallas kernels: 66 us -> 64.7 us
    pallas_call x1, Pallas kernels: 66 us -> 64.7 us  [shards(): pl.pallas_call(layer_kernel, out_shape=jax.ShapeDtypeStruct((r, w.shape[1...]
where the time goes in v5:
time: 65.5 us; the launch traced here: 65.4 us
  Pallas kernels  64.7 us (99%)
  local copies, waits for them, and re-layouts  0.68 us (1%)
    pallas_call x1, Pallas kernels, shards(): pl.pallas_call(layer_kernel, out_shape=jax.ShapeDtypeStruct((r, w.shape[1...  64.7 us

profile of v5, /device:TPU:1, one launch (start us, length us, event | category | flops | bytes accessed | tf_op | source)
XLA Modules:
  0.0 65.4 jit_solution(6546753125557912068)
XLA Ops:
  0.0 64.7 %layer.1 = bf16[48,2048]{1,0:T(8,128)(2,1)S(1)} custom-call(bf16[384,256]{1,0:T(8,128)(2,1)} %q.1, bf16[384,256]{1,0:T(8,128)(2,1)} %k.1, bf16[384,512]{1,0:T(8,128)(2,1)} %v.1, bf16[384,512]{1,0:T(8,128)(2,1)} %gate.1, f32[4,256]{1,0:T(4,128)} %qt.1, f32[4,256]{1,0:T(4,128)} %kt.1, f32[4,512]{1,0:T(4,128)} %vt.1, f32[4,384]{1,0:T(4,128)} %bitcast.3, ...), custom_call_target="tpu_custom_call" | custom-call | tf_op jit(solution)/shard_map/layer/pallas_call | solution.py:427
  64.7 0.7 %copy.13 = bf16[48,2048]{1,0:T(8,128)(2,1)} copy(bf16[48,2048]{1,0:T(8,128)(2,1)S(1)} %layer.1) | data formatting | bytes 393216

commit v6 on v5

--- a/solution.py
+++ b/solution.py
@@ -77,7 +77,7 @@
             device_id_type=MESH,
         )
 
-    out = [copy(off, lambda to: slot) for off in range(1, 4)]
+    out = [copy(off, lambda to: slot) for off in (2, 1, 3)]
     for c in out:
         c.start()
     return out, [copy(off, lambda to: to) for off in range(1, 4)]
@@ -101,6 +101,7 @@
     loads = {}
     for i, (src, dst) in enumerate(pairs_in):
         loads[i] = pltpu.make_async_copy(src, dst, in_sem.at[i])
+    for i in range(6):
         loads[i].start()
     me, l, g, x = place()
     hd = lax.axis_index("head")
@@ -175,8 +176,8 @@
         lo += ref.shape[1]
     for copy in sent_halo:
         copy.start()
-    sent_w = remote(w, w_sib, sw.at[0], rw.at[0], sibling)
-    sent_w.start()
+    for i in range(6, 11):
+        loads[i].start()
 
     def put(lo, raw):
         wide = raw.shape[1]
@@ -275,6 +276,8 @@
 
     c1, w1 = exchange(l, at_l, lambda i: pair.at[i], buf1, s1, r1)
     buf1[l] = pair[l]
+    sent_w = remote(w, w_sib, sw.at[0], rw.at[0], sibling)
+    sent_w.start()
 
     loads[6].wait()
     loads[7].wait()

time: 65.5 us -> 65.5 us (level)
  no operation moved by 1% of the time
where the time goes in v6:
time: 65.5 us; the launch traced here: 65.4 us
  Pallas kernels  64.7 us (99%)
  local copies, waits for them, and re-layouts  0.68 us (1%)
    pallas_call x1, Pallas kernels, shards(): pl.pallas_call(layer_kernel, out_shape=jax.ShapeDtypeStruct((r, w.shape[1...  64.7 us

profile of v6, /device:TPU:1, one launch (start us, length us, event | category | flops | bytes accessed | tf_op | source)
XLA Modules:
  0.0 65.4 jit_solution(14320282043245481855)
XLA Ops:
  0.0 64.7 %layer.1 = bf16[48,2048]{1,0:T(8,128)(2,1)S(1)} custom-call(bf16[384,256]{1,0:T(8,128)(2,1)} %q.1, bf16[384,256]{1,0:T(8,128)(2,1)} %k.1, bf16[384,512]{1,0:T(8,128)(2,1)} %v.1, bf16[384,512]{1,0:T(8,128)(2,1)} %gate.1, f32[4,256]{1,0:T(4,128)} %qt.1, f32[4,256]{1,0:T(4,128)} %kt.1, f32[4,512]{1,0:T(4,128)} %vt.1, f32[4,384]{1,0:T(4,128)} %bitcast.3, ...), custom_call_target="tpu_custom_call" | custom-call | tf_op jit(solution)/shard_map/layer/pallas_call | solution.py:430
  64.7 0.7 %copy.13 = bf16[48,2048]{1,0:T(8,128)(2,1)} copy(bf16[48,2048]{1,0:T(8,128)(2,1)S(1)} %layer.1) | data formatting | bytes 393216
